TPU v7x, 32 devices: a whole 2x2x4 slice. The times are simulated.
32 devices in a mesh: groups: 2 (over y), seq: 8 (over z, x), tensor: 2 (over core).
Axes of the slice: x: 2, y: 2, z: 4, core: 2. Of those that a mesh axis runs over, the one named last changes fastest.
Arguments:
- q_proj: bfloat16 [2048, 8192], P(('groups', 'seq'), 'tensor'), parts along dimension 0, may hold values from -6 to 6
- k_proj: bfloat16 [2048, 8192], P(('groups', 'seq'), 'tensor'), parts along dimension 0, may hold values from -6 to 6
- v_proj: bfloat16 [2048, 8192], P(('groups', 'seq'), 'tensor'), parts along dimension 0, may hold values from -6 to 6
- short_taps: bfloat16 [3, 7, 8192], P(None, None, 'tensor'), may hold values from -2 to 2
- pole_rate: float32 [16, 8192], P(None, 'tensor'), may hold values from 4.8828125e-05 to 0.0333333333
- pole_angle: float32 [16, 8192], P(None, 'tensor'), may hold values from -3.140625 to 3.140625
- residue_re: float32 [16, 8192], P(None, 'tensor'), may hold values from -0.3 to 0.3
- residue_im: float32 [16, 8192], P(None, 'tensor'), may hold values from -0.3 to 0.3
- skip_gain: float32 [8192], P('tensor'), may hold values from -3 to 3
Outputs:
- mixed_out: bfloat16 [2048, 8192], P(('groups', 'seq'), 'tensor'), parts along dimension 0
There are 2 independent parts, one for each index of `groups`. A program takes and returns all parts, laid end to end along the dimension named above; an argument that names none is the same for every part. Nothing has to cross between parts.
All inputs are finite; a program needn't handle non-finite values.
Results may differ from a plain program's by a relative error of at most 0.0049.
Values may be sent and summed in bfloat16 or wider, within the bound.
No kernel may reach another device: no remote copies, remote signals or barrier semaphores. Data moves between devices by JAX's collectives and lax.ppermute only.
A program may use at most 192 MiB of HBM per device.

v0:
```python
import functools

import jax
import jax.numpy as jnp
from jax import lax
from jax.experimental import pallas as pl
from jax.experimental.pallas import tpu as pltpu
from jax.sharding import PartitionSpec as P

F32 = jnp.float32
BF16 = jnp.bfloat16
LANES = 128
ROWS = 8
CHUNK = 16

SIN = (0.9999999999829191, -0.16666666616793607, 0.008333330972826632,
       -0.00019840860946827691, 2.752525553710695e-06, -2.3888929551921256e-08)
COS = (0.9999999997792479, -0.4999999935536099, 0.04166663614859566,
       -0.0013888360060282819, 2.4760094764212313e-05, -2.605034249002706e-07)


def cmul(ar, ai, br, bi):
    return ar * br - ai * bi, ar * bi + ai * br


def horner(coefs, u):
    total = jnp.full_like(u, coefs[-1])
    for coef in coefs[-2::-1]:
        total = total * u + coef
    return total


def pole(rate, angle):
    half = angle * 0.5
    square = half * half
    sin_half = half * horner(SIN, square)
    cos_half = horner(COS, square)
    size = jnp.exp(-rate)
    return size * (1.0 - 2.0 * sin_half * sin_half), size * (2.0 * sin_half * cos_half)


def conv_rows(padded, taps, at, rows):
    total = None
    for j, tap in enumerate(taps):
        term = tap * padded[pl.ds(ROWS + at - j, rows), :]
        total = term if total is None else total + term
    return total


def fill(padded, rim, rows_in, first):
    padded[pl.ds(0, ROWS), :] = jnp.where(first, 0.0, rim.astype(F32))
    padded[pl.ds(ROWS, rows_in.shape[0]), :] = rows_in.astype(F32)


def tap_rows(ref, branch, lanes, scratch):
    count = ref.shape[1]
    scratch[pl.ds(0, count), :] = ref[branch, :, lanes].astype(F32)
    return [scratch[pl.ds(j, 1), :] for j in range(count)]


def over_tiles(width, body):
    def visit(i, carry):
        body(pl.ds(pl.multiple_of(i * LANES, LANES), LANES))
        return carry

    lax.fori_loop(0, width // LANES, visit, 0)


def state_kernel(info, k_ref, v_ref, rim_ref, taps_ref, rate_ref, angle_ref, res_re_ref, res_im_ref,
                 gated_ref, chunk_ref, total_ref, lam_ref, span_ref, filt_ref,
                 pad_k, pad_v, gate, tap_k, tap_v):
    first = info[1] == 1
    length, width = k_ref.shape
    chunks = length // CHUNK

    def tile(lanes):
        fill(pad_k, rim_ref[1, :, lanes], k_ref[:, lanes], first)
        fill(pad_v, rim_ref[2, :, lanes], v_ref[:, lanes], first)
        taps_k = tap_rows(taps_ref, 1, lanes, tap_k)
        taps_v = tap_rows(taps_ref, 2, lanes, tap_v)
        for at in range(0, length, CHUNK):
            product = conv_rows(pad_k, taps_k, at, CHUNK) * conv_rows(pad_v, taps_v, at, CHUNK)
            rounded = product.astype(BF16)
            gated_ref[pl.ds(at, CHUNK), lanes] = rounded
            gate[pl.ds(at, CHUNK), :] = rounded.astype(F32)
        lam_re, lam_im = pole(rate_ref[:, lanes], angle_ref[:, lanes])
        lam_ref[0, :, lanes] = lam_re
        lam_ref[1, :, lanes] = lam_im
        weight_re, weight_im = res_re_ref[:, lanes], res_im_ref[:, lanes]
        filt_ref[pl.ds(0, 1), lanes] = jnp.sum(weight_re, axis=0, keepdims=True)
        zero = jnp.zeros_like(weight_re)
        sums = [(zero, zero)] * chunks
        for b in range(CHUNK - 1, -1, -1):
            weight_re, weight_im = cmul(weight_re, weight_im, lam_re, lam_im)
            if b:
                filt_ref[pl.ds(CHUNK - b, 1), lanes] = jnp.sum(weight_re, axis=0, keepdims=True)
            for a in range(chunks):
                row = gate[pl.ds(a * CHUNK + b, 1), :]
                sums[a] = (sums[a][0] + weight_re * row, sums[a][1] + weight_im * row)
        step_re, step_im = lam_re, lam_im
        reach = 1
        while reach < CHUNK:
            step_re, step_im = cmul(step_re, step_im, step_re, step_im)
            reach *= 2
        total_re, total_im = sums[0]
        for a in range(chunks):
            chunk_ref[a, 0, :, lanes] = sums[a][0]
            chunk_ref[a, 1, :, lanes] = sums[a][1]
            if a:
                moved_re, moved_im = cmul(step_re, step_im, total_re, total_im)
                total_re, total_im = moved_re + sums[a][0], moved_im + sums[a][1]
        total_ref[0, :, lanes] = total_re
        total_ref[1, :, lanes] = total_im
        while reach < length:
            step_re, step_im = cmul(step_re, step_im, step_re, step_im)
            reach *= 2
        span_ref[0, :, lanes] = step_re
        span_ref[1, :, lanes] = step_im

    over_tiles(width, tile)


def local_kernel(info, q_ref, rim_ref, taps_ref, gain_ref, gated_ref, filt_ref,
                 query_ref, local_ref, pad_q, gate, tap_q):
    first = info[1] == 1
    length, width = q_ref.shape
    chunks = length // CHUNK
    gate[...] = jnp.zeros_like(gate)

    def tile(lanes):
        fill(pad_q, rim_ref[0, :, lanes], q_ref[:, lanes], first)
        taps = tap_rows(taps_ref, 0, lanes, tap_q)
        for at in range(0, length, CHUNK):
            query_ref[pl.ds(at, CHUNK), lanes] = conv_rows(pad_q, taps, at, CHUNK)
        for a in range(chunks):
            gate[pl.ds(2 * CHUNK * a + CHUNK, CHUNK), :] = gated_ref[pl.ds(a * CHUNK, CHUNK), lanes].astype(F32)
        filt = [filt_ref[pl.ds(j, 1), lanes] for j in range(CHUNK)]
        filt[0] = filt[0] + gain_ref[:, lanes]
        for a in range(chunks):
            base = 2 * CHUNK * a + CHUNK
            for low in range(0, CHUNK, ROWS):
                total = None
                for j in range(low + ROWS):
                    term = filt[j] * gate[pl.ds(base + low - j, ROWS), :]
                    total = term if total is None else total + term
                local_ref[pl.ds(a * CHUNK + low, ROWS), lanes] = total

    over_tiles(width, tile)


def carried_kernel(info, enter_ref, chunk_ref, lam_ref, query_ref, local_ref, *rest):
    out_ref, pow_re, pow_im, coef_re, coef_im = rest[-5:]
    length, width = query_ref.shape
    modes = lam_ref.shape[1]
    chunks = length // CHUNK

    def tile(lanes):
        lam_re, lam_im = lam_ref[0, :, lanes], lam_ref[1, :, lanes]
        now_re, now_im = jnp.ones_like(lam_re), jnp.zeros_like(lam_re)
        for b in range(CHUNK):
            pow_re[pl.ds(b * modes, modes), :] = now_re
            pow_im[pl.ds(b * modes, modes), :] = now_im
            now_re, now_im = cmul(now_re, now_im, lam_re, lam_im) if b else (lam_re, lam_im)
        state_re, state_im = enter_ref[0, :, lanes], enter_ref[1, :, lanes]
        for a in range(chunks):
            coef_re[pl.ds(a * modes, modes), :] = state_re
            coef_im[pl.ds(a * modes, modes), :] = state_im
            if a + 1 < chunks:
                state_re, state_im = cmul(now_re, now_im, state_re, state_im)
                state_re, state_im = state_re + chunk_ref[a, 0, :, lanes], state_im + chunk_ref[a, 1, :, lanes]
        totals = [local_ref[pl.ds(a * CHUNK, CHUNK), lanes] for a in range(chunks)]
        for m in range(modes):
            u_re = pow_re[pl.ds(m, CHUNK, stride=modes), :]
            u_im = pow_im[pl.ds(m, CHUNK, stride=modes), :]
            for a in range(chunks):
                c_re = coef_re[pl.ds(a * modes + m, 1), :]
                c_im = coef_im[pl.ds(a * modes + m, 1), :]
                totals[a] = totals[a] + (u_re * c_re - u_im * c_im)
        for a in range(chunks):
            at = pl.ds(a * CHUNK, CHUNK)
            out_ref[at, lanes] = (query_ref[at, lanes] * totals[a]).astype(BF16)

    over_tiles(width, tile)


def block_width(half):
    width = LANES
    while width < 512 and half % (2 * width) == 0:
        width *= 2
    return width


def shards(
    q_proj, k_proj, v_proj, short_taps, pole_rate, pole_angle, residue_re, residue_im, skip_gain
):
    length, channels = q_proj.shape
    branches, short_len = short_taps.shape[:2]
    modes = pole_rate.shape[0]
    half = channels // 2
    width = block_width(half)
    blocks = half // width
    chunks = length // CHUNK
    axis_size = lax.axis_size("seq")
    index = lax.axis_index("seq")
    odd = index % 2 == 1

    tails = jnp.stack([branch[length - ROWS:] for branch in (q_proj, k_proj, v_proj)])
    rims = lax.ppermute(tails, "seq", [(i, (i + 1) % axis_size) for i in range(axis_size)])
    is_first = (index == 0).astype(jnp.int32)
    own = (index % 2).astype(jnp.int32)
    gain = skip_gain[None]

    def at_half(shape):
        lead = len(shape) - 1
        return pl.BlockSpec(shape, lambda i, info: (0,) * lead + (info[0] * blocks + i,))

    def in_half(shape):
        lead = len(shape) - 1
        return pl.BlockSpec(shape, lambda i, info: (0,) * lead + (i,))

    def call(kernel, info, in_specs, out_specs, out_shape, scratch, cost, aliases=None):
        return pl.pallas_call(
            kernel,
            out_shape=out_shape,
            grid_spec=pltpu.PrefetchScalarGridSpec(
                num_scalar_prefetch=1, grid=(blocks,), in_specs=in_specs, out_specs=out_specs,
                scratch_shapes=scratch,
            ),
            input_output_aliases=aliases or {},
            cost_estimate=pl.CostEstimate(flops=cost, bytes_accessed=cost, transcendentals=0),
        )

    def vmem(rows):
        return pltpu.VMEM((rows, LANES), F32)

    def shape(*dims, dtype=F32):
        return jax.ShapeDtypeStruct(dims, dtype)

    def states(info):
        return call(
            state_kernel,
            info,
            [at_half((length, width))] * 2
            + [at_half((branches, ROWS, width)), at_half((branches, short_len, width))]
            + [at_half((modes, width))] * 4,
            [in_half((length, width)), in_half((chunks, 2, modes, width))]
            + [in_half((2, modes, width))] * 3 + [in_half((CHUNK, width))],
            [shape(length, half, dtype=BF16), shape(chunks, 2, modes, half)]
            + [shape(2, modes, half)] * 3 + [shape(CHUNK, half)],
            [vmem(length + ROWS), vmem(length + ROWS), vmem(length), vmem(ROWS), vmem(ROWS)],
            1 << 20,
        )(info, k_proj, v_proj, rims, short_taps, pole_rate, pole_angle, residue_re, residue_im)

    def local(info, gated, filt):
        return call(
            local_kernel,
            info,
            [at_half((length, width)), at_half((branches, ROWS, width)), at_half((branches, short_len, width)),
             at_half((1, width)), in_half((length, width)), in_half((CHUNK, width))],
            [in_half((length, width))] * 2,
            [shape(length, half)] * 2,
            [vmem(length + ROWS), vmem(2 * length), vmem(ROWS)],
            1 << 20,
        )(info, q_proj, rims, short_taps, gain, gated, filt)

    def finish(info, enter, chunk, lam, query, near, out=None):
        args = [info, enter, chunk, lam, query, near]
        specs = [in_half((2, modes, width)), in_half((chunks, 2, modes, width)), in_half((2, modes, width)),
                 in_half((length, width)), in_half((length, width))]
        aliases = None
        if out is not None:
            args.append(out)
            specs.append(pl.BlockSpec(memory_space=pl.ANY))
            aliases = {len(args) - 1: 0}
        return call(
            carried_kernel, info, specs, at_half((length, width)), shape(length, channels, dtype=BF16),
            [vmem(CHUNK * modes), vmem(CHUNK * modes), vmem(chunks * modes), vmem(chunks * modes)],
            1 << 20, aliases,
        )(*args)

    def swap(block, distance):
        return lax.ppermute(block, "seq", [(i, i ^ distance) for i in range(axis_size)])

    def times(a, b):
        return jnp.stack(cmul(a[0], a[1], b[0], b[1]))

    info_own = jnp.stack([own, is_first])
    info_other = jnp.stack([1 - own, is_first])
    gated_o, chunk_o, total_o, lam_o, _, filt_o = states(info_other)
    from_mate = swap(total_o.astype(BF16), 1)
    gated_m, chunk_m, total_m, lam_m, span, filt_m = states(info_own)
    query_o, near_o = local(info_other, gated_o, filt_o)
    query_m, near_m = local(info_own, gated_m, filt_m)

    from_mate = from_mate.astype(F32)
    early = jnp.where(odd, from_mate, total_m)
    late = jnp.where(odd, total_m, from_mate)
    block = times(span, early) + late
    power = times(span, span)
    enter = jnp.zeros_like(block)
    decay = None
    distance = 2
    while distance < axis_size:
        arrived = swap(block.astype(BF16), distance).astype(F32)
        upper = (index & distance) != 0
        moved = arrived if decay is None else times(decay, arrived)
        enter = enter + jnp.where(upper, moved, 0.0)
        if 2 * distance < axis_size:
            block = times(power, jnp.where(upper, arrived, block)) + jnp.where(upper, block, arrived)
            one = jnp.stack([jnp.ones_like(power[0]), jnp.zeros_like(power[0])])
            grown = jnp.where(upper, power, one)
            decay = grown if decay is None else times(decay, grown)
            power = times(power, power)
        distance *= 2
    past = times(span, enter) + early
    handed = swap(jnp.where(odd, enter, past).astype(BF16), 1)
    mine = jnp.where(odd, past, enter)
    out = finish(info_own, mine, chunk_m, lam_m, query_m, near_m)
    return finish(info_other, handed.astype(F32), chunk_o, lam_o, query_o, near_o, out)


def solution(mesh):
    placed = (
        P(("groups", "seq"), "tensor"),
        P(("groups", "seq"), "tensor"),
        P(("groups", "seq"), "tensor"),
        P(None, None, "tensor"),
        P(None, "tensor"),
        P(None, "tensor"),
        P(None, "tensor"),
        P(None, "tensor"),
        P("tensor"),
    )
    return jax.shard_map(
        shards,
        mesh=mesh,
        in_specs=placed,
        out_specs=P(("groups", "seq"), "tensor"),
        check_vma=False,
    )
```

profile of v0, /device:TPU:0, one launch (start us, length us, event | category | flops | bytes accessed | tf_op | source)
XLA Modules:
  0.0 70.0 jit_solution(9736503174969091512)
XLA Ops:
  0.0 0.8 %slice_bitcast_fusion.2 = bf16[1,8,4096]{2,1,0:T(8,128)(2,1)S(1)} fusion(bf16[128,4096]{1,0:T(8,128)(2,1)} %q_ref.3), kind=kLoop, calls=%fused_computation.27 | loop fusion | bytes 131072 | tf_op jit(solution)/shard_map/stack | solution.py:207
  0.8 0.9 %slice_bitcast_fusion = (bf16[1,8,4096]{2,1,0:T(8,128)(2,1)S(1)}, bf16[1,8,4096]{2,1,0:T(8,128)(2,1)S(1)}) fusion(bf16[128,4096]{1,0:T(8,128)(2,1)} %v_ref.3, bf16[128,4096]{1,0:T(8,128)(2,1)} %k_ref.3), kind=kLoop, calls=%fused_computation.25 | loop fusion | bytes 262144 | tf_op jit(solution)/shard_map/stack | solution.py:207
  1.8 3.0 %collective-permute-start = (bf16[3,8,4096]{2,1,0:T(8,128)(2,1)S(1)}, bf16[3,8,4096]{2,1,0:T(8,128)(2,1)S(1)}, u32[]{:S(2)}, u32[]{:S(2)}) collective-permute-start(bf16[3,8,4096]{2,1,0:T(8,128)(2,1)S(1)} %pad_maximum_fusion), channel_id=1, source_target_pairs={{0,2},{2,4},{4,6},{6,8},{8,10},{10,12},{12,14},{14,0},{1,3},{3,5},... | collective-permute-start | bytes 589832 | tf_op jit(solution)/shard_map/ppermute | solution.py:208
  4.8 0.6 pad_add_fusion.info
  5.3 7.4 %collective-permute-done.rim_ref = bf16[3,8,4096]{2,1,0:T(8,128)(2,1)S(1)} collective-permute-done((bf16[3,8,4096]{2,1,0:T(8,128)(2,1)S(1)}, bf16[3,8,4096]{2,1,0:T(8,128)(2,1)S(1)}, u32[]{:S(2)}, u32[]{:S(2)}) %collective-permute-start) | collective-permute-done | bytes 196640 | tf_op jit(solution)/shard_map/ppermute | solution.py:208
  12.7 0.0 copy-start
  12.7 0.7 copy-done
  13.4 8.0 %shard_map.92 = (bf16[128,2048]{1,0:T(8,128)(2,1)}, f32[8,2,16,2048]{3,2,1,0:T(8,128)}, f32[2,16,2048]{2,1,0:T(8,128)}, f32[2,16,2048]{2,1,0:T(8,128)}, f32[2,16,2048]{2,1,0:T(8,128)}, /*index=5*/f32[16,2048]{1,0:T(8,128)}) custom-call(s32[2]{0:T(128)} %pad_add_fusion.info, bf16[128,4096]{1,0:T(8,128)(2,1)} %k_ref.3, bf16[128,4096]{1,0:T(8,128)(2,1)} %v_ref.3, ...), custom_call_target="tpu_custom_call" | custom-call | flops 1048576 | bytes 1048576 | tf_op jit(solution)/shard_map/pallas_call | solution.py:240
  21.4 1.0 %convert_element_type.25 = bf16[2,16,2048]{2,1,0:T(8,128)(2,1)S(1)} convert(f32[2,16,2048]{2,1,0:T(8,128)} %get-tuple-element.21) | non-fusion elementwise | flops 65536 | bytes 393216 | tf_op jit(solution)/shard_map/convert_element_type | solution.py:290
  22.4 0.1 collective-permute-start.1
  22.5 0.6 pad_add_fusion.1.info
  23.1 8.0 %shard_map.91 = (bf16[128,2048]{1,0:T(8,128)(2,1)}, f32[8,2,16,2048]{3,2,1,0:T(8,128)}, f32[2,16,2048]{2,1,0:T(8,128)}, f32[2,16,2048]{2,1,0:T(8,128)}, f32[2,16,2048]{2,1,0:T(8,128)}, /*index=5*/f32[16,2048]{1,0:T(8,128)}) custom-call(s32[2]{0:T(128)} %pad_add_fusion.1.info, bf16[128,4096]{1,0:T(8,128)(2,1)} %k_ref.3, bf16[128,4096]{1,0:T(8,128)(2,1)} %v_ref.3, ...), custom_call_target="tpu_custom_call" | custom-call | flops 1048576 | bytes 1048576 | tf_op jit(solution)/shard_map/pallas_call | solution.py:240
  31.1 0.0 collective-permute-done.1
  31.1 1.0 %convert_select_fusion.4 = f32[2,16,2048]{2,1,0:T(8,128)S(1)} fusion(f32[2,16,2048]{2,1,0:T(8,128)} %get-tuple-element.22, bf16[2,16,2048]{2,1,0:T(8,128)(2,1)S(1)} %collective-permute-done.1, pred[]{:T(512)S(6)} %eq.10), kind=kLoop, calls=%fused_computation.4 | loop fusion | flops 131072 | bytes 655361 | tf_op jit(solution)/shard_map/jit(_where)/select_n | solution.py:296
  32.1 1.0 %multiply_subtract_fusion.4 = (f32[1,16,2048]{2,1,0:T(8,128)S(1)}, f32[1,16,2048]{2,1,0:T(8,128)S(1)}) fusion(f32[2,16,2048]{2,1,0:T(8,128)S(1)} %convert_select_fusion.4, f32[2,16,2048]{2,1,0:T(8,128)} %get-tuple-element.20), kind=kLoop, calls=%fused_computation.23 | loop fusion | flops 196608 | bytes 786432 | tf_op jit(solution)/shard_map/sub | solution.py:23
  33.1 0.1 fusion.4
  33.2 0.3 collective-permute-start.2
  33.5 5.4 %shard_map.94 = (f32[128,2048]{1,0:T(8,128)}, f32[128,2048]{1,0:T(8,128)}) custom-call(s32[2]{0:T(128)} %pad_add_fusion.1.info, bf16[128,4096]{1,0:T(8,128)(2,1)} %q_ref.3, bf16[3,8,4096]{2,1,0:T(8,128)(2,1)} %copy-done, bf16[3,7,4096]{2,1,0:T(8,128)(2,1)} %taps_ref.7, f32[1,4096]{1,0:T(1,128)} %bitcast.10, bf16[128,2048]{1,0:T(8,128)(2,1)} %get-tuple-element.31.gated_ref, ...), custom_call_target="tpu_custom_call" | custom-call | flops 1048576 | bytes 1048576 | tf_op jit(solution)/shard_map/pallas_call | solution.py:255
  39.0 5.4 %shard_map.93 = (f32[128,2048]{1,0:T(8,128)}, f32[128,2048]{1,0:T(8,128)}) custom-call(s32[2]{0:T(128)} %pad_add_fusion.info, bf16[128,4096]{1,0:T(8,128)(2,1)} %q_ref.3, bf16[3,8,4096]{2,1,0:T(8,128)(2,1)} %copy-done, bf16[3,7,4096]{2,1,0:T(8,128)(2,1)} %taps_ref.7, f32[1,4096]{1,0:T(1,128)} %bitcast.11, bf16[128,2048]{1,0:T(8,128)(2,1)} %get-tuple-element.25.gated_ref, ...), custom_call_target="tpu_custom_call" | custom-call | flops 1048576 | bytes 1048576 | tf_op jit(solution)/shard_map/pallas_call | solution.py:255
  44.4 0.0 collective-permute-done.2
  44.4 0.0 copy-done.1
  44.4 0.1 multiply_subtract_fusion.2
  44.6 2.7 %collective-permute-start.3 = (bf16[2,16,2048]{2,1,0:T(8,128)(2,1)S(1)}, bf16[2,16,2048]{2,1,0:T(8,128)(2,1)S(1)}, u32[]{:S(2)}, u32[]{:S(2)}) collective-permute-start(bf16[2,16,2048]{2,1,0:T(8,128)(2,1)S(1)} %fusion.3), channel_id=1, source_target_pairs={{0,8},{2,10},{4,12},{6,14},{8,0},{10,2},{12,4},{14,6},{1,9},{3,11}... | collective-permute-start | bytes 393224 | tf_op jit(solution)/shard_map/ppermute | solution.py:282
  47.2 0.0 copy-done.2
  47.3 5.5 %collective-permute-done.3 = bf16[2,16,2048]{2,1,0:T(8,128)(2,1)S(1)} collective-permute-done((bf16[2,16,2048]{2,1,0:T(8,128)(2,1)S(1)}, bf16[2,16,2048]{2,1,0:T(8,128)(2,1)S(1)}, u32[]{:S(2)}, u32[]{:S(2)}) %collective-permute-start.3) | collective-permute-done | bytes 131104 | tf_op jit(solution)/shard_map/ppermute | solution.py:282
  52.9 0.1 select_convert_fusion
  53.0 1.8 %collective-permute-start.4 = (bf16[2,16,2048]{2,1,0:T(8,128)(2,1)S(1)}, bf16[2,16,2048]{2,1,0:T(8,128)(2,1)S(1)}, u32[]{:S(2)}, u32[]{:S(2)}) collective-permute-start(bf16[2,16,2048]{2,1,0:T(8,128)(2,1)S(1)} %select_convert_fusion), channel_id=1, source_target_pairs={{0,2},{2,0},{4,6},{6,4},{8,10},{10,8},{12,14},{14,12},{1,3},{3,1},... | collective-permute-start | bytes 393224 | tf_op jit(solution)/shard_map/ppermute | solution.py:282
  54.8 0.8 %broadcast_select_fusion.enter_ref = f32[2,16,2048]{2,1,0:T(8,128)} fusion(pred[]{:T(512)S(6)} %eq.10, f32[2,16,2048]{2,1,0:T(8,128)S(1)} %convert_select_fusion.4, f32[1,16,2048]{2,1,0:T(8,128)S(1)} %get-tuple-element.41, f32[1,16,2048]{2,1,0:T(8,128)S(1)} %get-tuple-element.40, f32[1,16,2048]{2,1,0:T(8,128)S(1)} %get-tuple-element.43, ...), kind=kLoop, calls=%fused_computation.24 | loop fusion | flops 524288 | bytes 1179651 | tf_op jit(solution)/shard_map/jit(_where)/select_n | solution.py:317
  55.6 6.8 %shard_map.95.rest_0_ = bf16[128,4096]{1,0:T(8,128)(2,1)} custom-call(s32[2]{0:T(128)} %pad_add_fusion.1.info, f32[2,16,2048]{2,1,0:T(8,128)} %broadcast_select_fusion.enter_ref, f32[8,2,16,2048]{3,2,1,0:T(8,128)} %get-tuple-element.29.chunk_ref, f32[2,16,2048]{2,1,0:T(8,128)} %get-tuple-element.30.lam_ref, f32[128,2048]{1,0:T(8,128)} %get-tuple-element.33.query_ref, ...), custom_call_target="tpu_custom_call" | custom-call | flops 1048576 | bytes 1048576 | tf_op jit(solution)/shard_map/pallas_call | solution.py:275
  62.4 0.0 collective-permute-done.4
  62.4 0.7 %convert_element_type.32.enter_ref = f32[2,16,2048]{2,1,0:T(8,128)} convert(bf16[2,16,2048]{2,1,0:T(8,128)(2,1)S(1)} %collective-permute-done.4) | non-fusion elementwise | flops 65536 | bytes 393216 | tf_op jit(solution)/shard_map/convert_element_type | solution.py:319
  63.1 6.8 %shard_map.96 = bf16[128,4096]{1,0:T(8,128)(2,1)} custom-call(s32[2]{0:T(128)} %pad_add_fusion.info, f32[2,16,2048]{2,1,0:T(8,128)} %convert_element_type.32.enter_ref, f32[8,2,16,2048]{3,2,1,0:T(8,128)} %get-tuple-element.23.chunk_ref, f32[2,16,2048]{2,1,0:T(8,128)} %get-tuple-element.24.lam_ref, ...), custom_call_target="tpu_custom_call", output_to_operand_aliasing={{}: (6, {})} | custom-call | flops 1048576 | bytes 1048576 | tf_op jit(solution)/shard_map/pallas_call | solution.py:275
  (11 shorter events, 0.3 us)
Async XLA Ops:
  1.8 11.0 %collective-permute-start = (bf16[3,8,4096]{2,1,0:T(8,128)(2,1)S(1)}, bf16[3,8,4096]{2,1,0:T(8,128)(2,1)S(1)}, u32[]{:S(2)}, u32[]{:S(2)}) collective-permute-start(bf16[3,8,4096]{2,1,0:T(8,128)(2,1)S(1)} %pad_maximum_fusion), channel_id=1, source_target_pairs={{0,2},{2,4},{4,6},{6,8},{8,10},{10,12},{12,14},{14,0},{1,3},{3,5},... | collective-permute-start | bytes 589832 | tf_op jit(solution)/shard_map/ppermute | solution.py:208
  12.7 0.7 copy-start
  22.4 8.7 %collective-permute-start.1 = (bf16[2,16,2048]{2,1,0:T(8,128)(2,1)S(1)}, bf16[2,16,2048]{2,1,0:T(8,128)(2,1)S(1)}, u32[]{:S(2)}, u32[]{:S(2)}) collective-permute-start(bf16[2,16,2048]{2,1,0:T(8,128)(2,1)S(1)} %convert_element_type.25), channel_id=1, source_target_pairs={{0,2},{2,0},{4,6},{6,4},{8,10},{10,8},{12,14},{14,12},{1,3},{3,1},... | collective-permute-start | bytes 393224 | tf_op jit(solution)/shard_map/ppermute | solution.py:282
  33.2 11.2 %collective-permute-start.2 = (bf16[2,16,2048]{2,1,0:T(8,128)(2,1)S(1)}, bf16[2,16,2048]{2,1,0:T(8,128)(2,1)S(1)}, u32[]{:S(2)}, u32[]{:S(2)}) collective-permute-start(bf16[2,16,2048]{2,1,0:T(8,128)(2,1)S(1)} %get-tuple-element.38), channel_id=1, source_target_pairs={{0,4},{2,6},{4,0},{6,2},{8,12},{10,14},{12,8},{14,10},{1,5},{3,7},... | collective-permute-start | bytes 393224 | tf_op jit(solution)/shard_map/ppermute | solution.py:282
  33.5 10.9 %copy-start.1 = (f32[2,16,2048]{2,1,0:T(8,128)S(1)}, f32[2,16,2048]{2,1,0:T(8,128)}, u32[]{:S(2)}) copy-start(f32[2,16,2048]{2,1,0:T(8,128)} %get-tuple-element.20) | copy-start | bytes 786436
  39.0 8.3 %copy-start.2 = (f32[2,16,2048]{2,1,0:T(8,128)S(1)}, f32[2,16,2048]{2,1,0:T(8,128)}, u32[]{:S(2)}) copy-start(f32[2,16,2048]{2,1,0:T(8,128)} %constant.28.clone.1) | copy-start | bytes 786436
  44.6 8.2 %collective-permute-start.3 = (bf16[2,16,2048]{2,1,0:T(8,128)(2,1)S(1)}, bf16[2,16,2048]{2,1,0:T(8,128)(2,1)S(1)}, u32[]{:S(2)}, u32[]{:S(2)}) collective-permute-start(bf16[2,16,2048]{2,1,0:T(8,128)(2,1)S(1)} %fusion.3), channel_id=1, source_target_pairs={{0,8},{2,10},{4,12},{6,14},{8,0},{10,2},{12,4},{14,6},{1,9},{3,11}... | collective-permute-start | bytes 393224 | tf_op jit(solution)/shard_map/ppermute | solution.py:282
  53.0 9.4 %collective-permute-start.4 = (bf16[2,16,2048]{2,1,0:T(8,128)(2,1)S(1)}, bf16[2,16,2048]{2,1,0:T(8,128)(2,1)S(1)}, u32[]{:S(2)}, u32[]{:S(2)}) collective-permute-start(bf16[2,16,2048]{2,1,0:T(8,128)(2,1)S(1)} %select_convert_fusion), channel_id=1, source_target_pairs={{0,2},{2,0},{4,6},{6,4},{8,10},{10,8},{12,14},{14,12},{1,3},{3,1},... | collective-permute-start | bytes 393224 | tf_op jit(solution)/shard_map/ppermute | solution.py:282
where the time goes:
time: 70.7 us; the launch traced here: 70 us
  Pallas kernels  40.6 us (57%)
  waiting for transfers between devices  12.9 us (18%)
  starting transfers between devices  7.85 us (11%)
  other arithmetic  6.1 us (9%)
  local copies, waits for them, and re-layouts  2.42 us (3%)
    pallas_call x2, Pallas kernels, states(): call(state_kernel, info, [at_half((length, width))] * 2 + [at_half((branc...  16.1 us
    pallas_call x2, Pallas kernels, finish(): call(carried_kernel, info, specs, at_half((length, width)), shape(length,...  13.7 us
    pallas_call x2, Pallas kernels, local(): call(local_kernel, info, [at_half((length, width)), at_half((branches, RO...  10.8 us
    ppermute x1, waiting for transfers between devices, shards(): lax.ppermute(tails, 'seq', [(i, (i + 1) % axis_size) for i in range(axis_...  7.38 us
    ppermute x4, waiting for transfers between devices, swap(): lax.ppermute(block, 'seq', [(i, i ^ distance) for i in range(axis_size)])  5.53 us
    ppermute x4, starting transfers between devices, swap(): lax.ppermute(block, 'seq', [(i, i ^ distance) for i in range(axis_size)])  4.83 us
    ppermute x1, starting transfers between devices, shards(): lax.ppermute(tails, 'seq', [(i, (i + 1) % axis_size) for i in range(axis_...  3.02 us
    another operation x2, local copies, waits for them, and re-layouts, shards(): jnp.stack([branch[length - ROWS:] for branch in (q_proj, k_proj, v_proj)])  1.72 us
  transfers between devices with their start and end apart: 5, of which 2 were waited for; matrix products, arithmetic and copies ran while one was open for 3% of the time, Pallas kernels for 37%

commit v1 on v0

v1 whole, which is shorter than its diff:
```python
import functools
import math

import jax
import jax.numpy as jnp
from jax import lax
from jax.experimental import pallas as pl
from jax.experimental.pallas import tpu as pltpu
from jax.sharding import PartitionSpec as P

F32 = jnp.float32
BF16 = jnp.bfloat16
LANES = 128
ROWS = 8
CHUNK = 16

SIN = (0.9999999999829191, -0.16666666616793607, 0.008333330972826632,
       -0.00019840860946827691, 2.752525553710695e-06, -2.3888929551921256e-08)
COS = (0.9999999997792479, -0.4999999935536099, 0.04166663614859566,
       -0.0013888360060282819, 2.4760094764212313e-05, -2.605034249002706e-07)


def cmul(ar, ai, br, bi):
    return ar * br - ai * bi, ar * bi + ai * br


def horner(coefs, u):
    total = jnp.full_like(u, coefs[-1])
    for coef in coefs[-2::-1]:
        total = total * u + coef
    return total


def pole(rate, angle):
    half = angle * 0.5
    square = half * half
    sin_half = half * horner(SIN, square)
    cos_half = horner(COS, square)
    size = jnp.exp(-rate)
    return size * (1.0 - 2.0 * sin_half * sin_half), size * (2.0 * sin_half * cos_half)


def conv_rows(padded, taps, at, rows):
    total = None
    for j, tap in enumerate(taps):
        term = tap * padded[pl.ds(ROWS + at - j, rows), :]
        total = term if total is None else total + term
    return total


def tap_rows(ref, branch, lanes, scratch):
    count = ref.shape[1]
    scratch[pl.ds(0, count), :] = ref[branch, :, lanes].astype(F32)
    return [scratch[pl.ds(j, 1), :] for j in range(count)]


def aligned(start):
    return pl.ds(pl.multiple_of(start, LANES), LANES)


def over_tiles(width, base, body):
    def visit(i, carry):
        body(aligned(base + i * LANES), aligned(i * LANES))
        return carry

    lax.fori_loop(0, width // LANES, visit, 0)


def half_start(width, mine):
    index = lax.axis_index("seq")
    parity = lax.rem(index, 2)
    return index == 0, (parity if mine else 1 - parity) * width


def power_of(re, im, doublings):
    for _ in range(doublings):
        re, im = cmul(re, im, re, im)
    return re, im


def gate_rows(pad_k, pad_v, taps_k, taps_v, at, gated_ref, lanes, gate):
    product = conv_rows(pad_k, taps_k, at, CHUNK) * conv_rows(pad_v, taps_v, at, CHUNK)
    rounded = product.astype(BF16)
    gated_ref[pl.ds(at, CHUNK), lanes] = rounded
    gate[pl.ds(at, CHUNK), :] = rounded.astype(F32)


def chunk_sums(gate, chunks, lam_re, lam_im):
    twice = lam_re + lam_re
    square = lam_re * lam_re + lam_im * lam_im
    older, newer = [None] * len(chunks), [None] * len(chunks)
    for b in range(CHUNK):
        for n, a in enumerate(chunks):
            now = gate[pl.ds(a * CHUNK + b, 1), :]
            if b == 0:
                now = jnp.broadcast_to(now, lam_re.shape)
            if b > 1:
                now = now - square * older[n]
            if b > 0:
                now = now + twice * newer[n]
            older[n], newer[n] = newer[n], now
    return [(new - lam_re * old, lam_im * old) for old, new in zip(older, newer)]


def put(ref, lanes, pair, *at):
    ref[(*at, 0, slice(None), lanes)] = pair[0].astype(ref.dtype)
    ref[(*at, 1, slice(None), lanes)] = pair[1].astype(ref.dtype)


def get(ref, lanes, *at):
    return ref[(*at, 0, slice(None), lanes)].astype(F32), ref[(*at, 1, slice(None), lanes)].astype(F32)


def add(a, b):
    return a[0] + b[0], a[1] + b[1]


def states_kernel(with_rim, *refs):
    refs = list(refs)
    k_ref, v_ref = refs[:2]
    rim_ref = refs.pop(2) if with_rim else None
    taps_ref, rate_ref, angle_ref = refs[2:5]
    gated_ref, chunk_ref, total_ref, lam_ref, step_ref, span_ref, pad_k, pad_v, gate, tap_k, tap_v = refs[5:]
    length = k_ref.shape[0]
    width = gated_ref.shape[1]
    first, base = half_start(width, with_rim)
    chunks = list(range(0 if with_rim else 1, length // CHUNK))

    def tile(full, half):
        for pad, ref, branch in ((pad_k, k_ref, 1), (pad_v, v_ref, 2)):
            if with_rim:
                pad[pl.ds(0, ROWS), :] = jnp.where(first, 0.0, rim_ref[branch, :, full].astype(F32))
            pad[pl.ds(ROWS, length), :] = ref[:, full].astype(F32)
        taps_k = tap_rows(taps_ref, 1, full, tap_k)
        taps_v = tap_rows(taps_ref, 2, full, tap_v)
        for a in chunks:
            gate_rows(pad_k, pad_v, taps_k, taps_v, a * CHUNK, gated_ref, half, gate)
        lam = pole(rate_ref[:, full], angle_ref[:, full])
        put(lam_ref, half, lam)
        sums = chunk_sums(gate, chunks, *lam)
        step = power_of(*lam, CHUNK.bit_length() - 1)
        put(step_ref, half, step)
        total = sums[0]
        for a, chunk in zip(chunks, sums):
            put(chunk_ref, half, chunk, a)
            if a != chunks[0]:
                total = add(cmul(*step, *total), chunk)
        put(total_ref, half, total)
        if with_rim:
            put(span_ref, half, power_of(*step, (length // CHUNK).bit_length() - 1))
        else:
            far, grown = None, step
            count = length // CHUNK - 1
            while count:
                if count % 2:
                    far = grown if far is None else cmul(*far, *grown)
                count //= 2
                if count:
                    grown = cmul(*grown, *grown)
            put(span_ref, half, far)

    over_tiles(width, base, tile)


def head_kernel(k_ref, v_ref, rim_ref, taps_ref, lam_ref, far_ref, rest_ref, gated_in, chunk_in,
                gated_ref, chunk_ref, total_ref, pad_k, pad_v, gate, tap_k, tap_v):
    del gated_in, chunk_in
    width = gated_ref.shape[1]
    first, base = half_start(width, False)

    def tile(full, half):
        for pad, ref, branch in ((pad_k, k_ref, 1), (pad_v, v_ref, 2)):
            pad[pl.ds(0, ROWS), :] = jnp.where(first, 0.0, rim_ref[branch, :, full].astype(F32))
            pad[pl.ds(ROWS, CHUNK), :] = ref[pl.ds(0, CHUNK), full].astype(F32)
        taps_k = tap_rows(taps_ref, 1, full, tap_k)
        taps_v = tap_rows(taps_ref, 2, full, tap_v)
        gate_rows(pad_k, pad_v, taps_k, taps_v, 0, gated_ref, half, gate)
        (chunk,) = chunk_sums(gate, [0], *get(lam_ref, half))
        put(chunk_ref, half, chunk, 0)
        put(total_ref, half, add(get(rest_ref, half), cmul(*get(far_ref, half), *chunk)))

    over_tiles(width, base, tile)


def local_kernel(mine, q_ref, rim_ref, taps_ref, gain_ref, res_re_ref, res_im_ref, lam_ref, gated_ref,
                 query_ref, local_ref, pow_ref, pad_q, gate, tap_q, table_re, table_im, line, mix):
    length = q_ref.shape[0]
    width = gated_ref.shape[1]
    modes = lam_ref.shape[1]
    first, base = half_start(width, mine)
    chunks = length // CHUNK
    side = ROWS // 2
    groups = modes // side
    for a in range(chunks):
        gate[pl.ds(2 * CHUNK * a, CHUNK), :] = jnp.zeros((CHUNK, LANES), F32)

    def tile(full, half):
        pad_q[pl.ds(0, ROWS), :] = jnp.where(first, 0.0, rim_ref[0, :, full].astype(F32))
        pad_q[pl.ds(ROWS, length), :] = q_ref[:, full].astype(F32)
        taps = tap_rows(taps_ref, 0, full, tap_q)
        for at in range(0, length, CHUNK):
            query_ref[pl.ds(at, CHUNK), half] = conv_rows(pad_q, taps, at, CHUNK)
        for a in range(chunks):
            gate[pl.ds(2 * CHUNK * a + CHUNK, CHUNK), :] = gated_ref[pl.ds(a * CHUNK, CHUNK), half].astype(F32)
        lam = get(lam_ref, half)
        res = res_re_ref[:, full], res_im_ref[:, full]
        even = cmul(*res, *lam)
        odd = cmul(*even, *lam)
        two = cmul(*lam, *lam)
        for n, part in enumerate((*even, *odd, *two)):
            line[pl.ds(n * modes, modes), :] = part
        for g in range(groups):
            for n, sources in enumerate(((0, 2), (1, 3), (4, 4), (5, 5))):
                for m, source in enumerate(sources):
                    at = (n * groups + g) * ROWS + m * side
                    mix[pl.ds(at, side), :] = line[pl.ds(source * modes + g * side, side), :]
        for g in range(groups):
            now_re, now_im, by_re, by_im = (mix[pl.ds((n * groups + g) * ROWS, ROWS), :] for n in range(4))
            for j in range(0, CHUNK, 2):
                at = pl.ds((g * CHUNK + j) * side, ROWS)
                table_re[at, :] = now_re
                table_im[at, :] = now_im
                if j + 2 < CHUNK:
                    now_re, now_im = cmul(now_re, now_im, by_re, by_im)
        later = None
        for m in range(modes):
            at = pl.ds(m // side * CHUNK * side + m % side, CHUNK, stride=side)
            u_re = table_re[at, :]
            pow_ref[0, m, :, half] = u_re
            pow_ref[1, m, :, half] = table_im[at, :]
            later = u_re if later is None else later + u_re
        line[pl.ds(0, CHUNK), :] = later
        filt = [jnp.sum(res[0], axis=0, keepdims=True) + gain_ref[:, full]]
        filt += [line[pl.ds(j, 1), :] for j in range(CHUNK - 1)]
        filt[0] = jnp.broadcast_to(filt[0], (ROWS, LANES))
        for a in range(chunks):
            start = 2 * CHUNK * a + CHUNK
            for low in range(0, CHUNK, ROWS):
                total = None
                for j in range(low + ROWS):
                    term = filt[j] * gate[pl.ds(start + low - j, ROWS), :]
                    total = term if total is None else total + term
                local_ref[pl.ds(a * CHUNK + low, ROWS), half] = total

    over_tiles(width, base, tile)


def carried_kernel(mine, enter_ref, chunk_ref, step_ref, pow_ref, query_ref, local_ref, *rest):
    out_ref, coef_re, coef_im, stage, sems = rest[-5:]
    length, width = query_ref.shape
    modes = step_ref.shape[1]
    chunks = length // CHUNK
    base = half_start(width, mine)[1]
    pieces = sems.shape[0]
    span = width // pieces

    def tile(half):
        step = get(step_ref, half)
        state = get(enter_ref, half)
        for a in range(chunks):
            coef_re[pl.ds(a * modes, modes), :] = state[0]
            coef_im[pl.ds(a * modes, modes), :] = state[1]
            if a + 1 < chunks:
                state = add(cmul(*step, *state), get(chunk_ref, half, a))
        totals = [local_ref[pl.ds(a * CHUNK, CHUNK), half] for a in range(chunks)]
        for m in range(modes):
            u_re = pow_ref[0, m, :, half]
            u_im = pow_ref[1, m, :, half]
            for a in range(chunks):
                c_re = coef_re[pl.ds(a * modes + m, 1), :]
                c_im = coef_im[pl.ds(a * modes + m, 1), :]
                totals[a] = totals[a] + (u_re * c_re - u_im * c_im)
        for a in range(chunks):
            at = pl.ds(a * CHUNK, CHUNK)
            stage[at, half] = (query_ref[at, half] * totals[a]).astype(BF16)

    def copy(piece):
        here = pl.ds(pl.multiple_of(piece * span, LANES), span)
        there = pl.ds(pl.multiple_of(base + piece * span, LANES), span)
        return pltpu.make_async_copy(stage.at[:, here], out_ref.at[:, there], sems.at[piece])

    def visit(piece, carry):
        def inner(i, carry):
            tile(aligned(piece * span + i * LANES))
            return carry

        lax.fori_loop(0, span // LANES, inner, 0)
        copy(piece).start()
        return carry

    lax.fori_loop(0, pieces, visit, 0)
    for piece in range(pieces):
        copy(piece).wait()


def tails_kernel(*refs):
    count = (len(refs) - 2) // 1
    sources, out_ref, sems = refs[:count], refs[count], refs[count + 1]
    copies = [
        pltpu.make_async_copy(ref.at[pl.ds(ref.shape[0] - ROWS, ROWS), :], out_ref.at[n], sems.at[n])
        for n, ref in enumerate(sources)
    ]
    for copy in copies:
        copy.start()
    for copy in copies:
        copy.wait()


def shards(
    q_proj, k_proj, v_proj, short_taps, pole_rate, pole_angle, residue_re, residue_im, skip_gain
):
    length, channels = q_proj.shape
    branches, short_len = short_taps.shape[:2]
    modes = pole_rate.shape[0]
    half = channels // 2
    chunks = length // CHUNK
    axis_size = lax.axis_size("seq")
    index = lax.axis_index("seq")
    odd = index % 2 == 1
    inside = pl.BlockSpec(memory_space=pltpu.VMEM)
    outside = pl.BlockSpec(memory_space=pl.ANY)

    def near(array):
        return pltpu.with_memory_space_constraint(array, pltpu.VMEM)

    def call(kernel, args, outs, scratch, cost, aliases=None, in_specs=None, out_specs=None):
        return pl.pallas_call(
            kernel,
            out_shape=outs,
            in_specs=in_specs or [inside] * len(args),
            out_specs=out_specs or ([inside] * len(outs) if isinstance(outs, list) else inside),
            scratch_shapes=scratch,
            input_output_aliases=aliases or {},
            compiler_params=pltpu.CompilerParams(vmem_limit_bytes=4 << 20),
            cost_estimate=pl.CostEstimate(flops=cost, bytes_accessed=cost, transcendentals=0),
        )(*args)

    def rows(count):
        return pltpu.VMEM((count, LANES), F32)

    def modal(dtype=F32):
        return pltpu.VMEM((2, modes, half), dtype)

    def swap(block, distance):
        return lax.ppermute(block, "seq", [(i, i ^ distance) for i in range(axis_size)])

    def times(a, b):
        return jnp.stack(cmul(a[0], a[1], b[0], b[1]))

    gates = pltpu.VMEM((length, half), BF16)
    sums = pltpu.VMEM((chunks, 2, modes, half), F32)
    pads = [rows(length + ROWS), rows(length + ROWS), rows(length), rows(ROWS), rows(ROWS)]

    tails = call(
        tails_kernel, [q_proj, k_proj, v_proj], pltpu.VMEM((branches, ROWS, channels), q_proj.dtype),
        [pltpu.SemaphoreType.DMA((branches,))], 1 << 16, in_specs=[outside] * branches,
    )
    rims = lax.ppermute(tails, "seq", [(i, (i + 1) % axis_size) for i in range(axis_size)])
    q, k, v, taps, rate, angle, res_re, res_im, gain = (
        near(array) for array in (
            q_proj, k_proj, v_proj, short_taps, pole_rate, pole_angle, residue_re, residue_im, skip_gain[None]
        )
    )

    gated_o, chunk_o, rest_o, lam_o, step_o, far_o = call(
        functools.partial(states_kernel, False), [k, v, taps, rate, angle],
        [gates, sums, modal(), modal(), modal(), modal()], pads, 16 << 20,
    )
    gated_o, chunk_o, total_o = call(
        head_kernel, [k, v, near(rims), taps, near(lam_o), near(far_o), near(rest_o), near(gated_o), near(chunk_o)],
        [gates, sums, modal(BF16)],
        [rows(CHUNK + ROWS), rows(CHUNK + ROWS), rows(CHUNK), rows(ROWS), rows(ROWS)],
        2 << 20, aliases={7: 0, 8: 1},
    )
    from_mate = swap(total_o, 1)
    gated_m, chunk_m, total_m, lam_m, step_m, span = call(
        functools.partial(states_kernel, True), [k, v, near(rims), taps, rate, angle],
        [gates, sums, modal(), modal(), modal(), modal()], pads, 16 << 20,
    )

    def local(mine, lam, gated):
        return call(
            functools.partial(local_kernel, mine),
            [q, near(rims), taps, gain, res_re, res_im, near(lam), near(gated)],
            [pltpu.VMEM((length, half), F32), pltpu.VMEM((length, half), F32), pltpu.VMEM((2, modes, CHUNK, half), F32)],
            [rows(length + ROWS), rows(2 * length), rows(ROWS), rows(CHUNK * modes), rows(CHUNK * modes),
             rows(6 * modes), rows(8 * modes)],
            8 << 20,
        )

    def finish(mine, enter, chunk, step, made, out=None):
        query, close, power = made
        args = [near(array) for array in (enter, chunk, step, power, query, close)]
        specs = [inside] * len(args)
        aliases = None
        if out is not None:
            args.append(out)
            specs.append(outside)
            aliases = {len(args) - 1: 0}
        pieces = math.gcd(half // LANES, 4)
        return call(
            functools.partial(carried_kernel, mine), args, jax.ShapeDtypeStruct((length, channels), BF16),
            [rows(chunks * modes), rows(chunks * modes), pltpu.VMEM((length, half), BF16),
             pltpu.SemaphoreType.DMA((pieces,))],
            8 << 20, aliases, specs, outside,
        )

    from_mate = from_mate.astype(F32)
    early = jnp.where(odd, from_mate, total_m)
    late = jnp.where(odd, total_m, from_mate)
    block = times(span, early) + late
    made_o = local(False, lam_o, gated_o)
    made_m = None
    power = times(span, span)
    enter = jnp.zeros_like(block)
    decay = None
    distance = 2
    while distance < axis_size:
        arrived = swap(block.astype(BF16), distance).astype(F32)
        upper = (index & distance) != 0
        moved = arrived if decay is None else times(decay, arrived)
        enter = enter + jnp.where(upper, moved, 0.0)
        if 2 * distance < axis_size:
            block = times(power, jnp.where(upper, arrived, block)) + jnp.where(upper, block, arrived)
            one = jnp.stack([jnp.ones_like(power[0]), jnp.zeros_like(power[0])])
            grown = jnp.where(upper, power, one)
            decay = grown if decay is None else times(decay, grown)
            power = times(power, power)
            if made_m is None:
                gated_m, block = lax.optimization_barrier((gated_m, block))
                made_m = local(True, lam_m, gated_m)
        distance *= 2
    if made_m is None:
        made_m = local(True, lam_m, gated_m)
    past = times(span, enter) + early
    handed = swap(jnp.where(odd, enter, past).astype(BF16), 1)
    mine = jnp.where(odd, past, enter)
    out = finish(True, mine, chunk_m, step_m, made_m)
    return finish(False, handed, chunk_o, step_o, made_o, out)


def solution(mesh):
    placed = (
        P(("groups", "seq"), "tensor"),
        P(("groups", "seq"), "tensor"),
        P(("groups", "seq"), "tensor"),
        P(None, None, "tensor"),
        P(None, "tensor"),
        P(None, "tensor"),
        P(None, "tensor"),
        P(None, "tensor"),
        P("tensor"),
    )
    return jax.shard_map(
        shards,
        mesh=mesh,
        in_specs=placed,
        out_specs=P(("groups", "seq"), "tensor"),
        check_vma=False,
    )
```

time: 70.7 us -> 58.5 us (0.83)
  Pallas kernels: 40.6 us -> 24 us
  local copies, waits for them, and re-layouts: 2.42 us -> 11.3 us
  waiting for transfers between devices: 12.9 us -> 7.79 us
  other arithmetic: 6.1 us -> 8.15 us
  starting transfers between devices: 7.85 us -> 6.46 us
    pallas_call x6 -> x8, Pallas kernels: 40.6 us -> 24 us  [call(): pl.pallas_call(kernel, out_shape=outs, in_specs=in_specs or [inside] * le...]
    unnamed x6 -> x72, local copies, waits for them, and re-layouts: 0.69 us -> 11.3 us
    ppermute x1, waiting for transfers between devices: 7.38 us -> 3.11 us  [shards(): lax.ppermute(tails, 'seq', [(i, (i + 1) % axis_size) for i in range(axis_...]
    another operation x2 -> x0, local copies, waits for them, and re-layouts: 1.72 us -> none  [shards(): jnp.stack([branch[length - ROWS:] for branch in (q_proj, k_proj, v_proj)])]
    convert_element_type x2 -> x0, other arithmetic: 1.7 us -> none  [the longest x1 0.97 us: shards(): from_mate = swap(total_o.astype(BF16), 1)]
    convert_element_type x3 -> x2, other arithmetic: 0.12 us -> 1.79 us  [shards(): arrived = swap(block.astype(BF16), distance).astype(F32)]
    ppermute x4, starting transfers between devices: 4.83 us -> 3.44 us  [swap(): lax.ppermute(block, 'seq', [(i, i ^ distance) for i in range(axis_size)])]
    another operation x3 -> x0, other arithmetic: 1.2 us -> none  [the longest x1 0.62 us: shards(): info_own = jnp.stack([own, is_first])]
  transfers between devices with their start and end apart: 5 -> 5, of which waited for: 2 -> 3; matrix products, arithmetic and copies ran while one was open for 3% -> 2% of each run, Pallas kernels for 37% -> 32%
where the time goes in v1:
time: 58.5 us; the launch traced here: 58 us
  Pallas kernels  24 us (41%)
  local copies, waits for them, and re-layouts  11.3 us (19%)
  other arithmetic  8.15 us (14%)
  waiting for transfers between devices  7.79 us (13%)
  starting transfers between devices  6.46 us (11%)
    pallas_call x8, Pallas kernels, call(): pl.pallas_call(kernel, out_shape=outs, in_specs=in_specs or [inside] * le...  24 us
    unnamed x72, local copies, waits for them, and re-layouts  11.3 us
    ppermute x4, waiting for transfers between devices, swap(): lax.ppermute(block, 'seq', [(i, i ^ distance) for i in range(axis_size)])  4.67 us
    ppermute x4, starting transfers between devices, swap(): lax.ppermute(block, 'seq', [(i, i ^ distance) for i in range(axis_size)])  3.44 us
    ppermute x1, waiting for transfers between devices, shards(): lax.ppermute(tails, 'seq', [(i, (i + 1) % axis_size) for i in range(axis_...  3.11 us
    ppermute x1, starting transfers between devices, shards(): lax.ppermute(tails, 'seq', [(i, (i + 1) % axis_size) for i in range(axis_...  3.02 us
    convert_element_type x2, other arithmetic, shards(): arrived = swap(block.astype(BF16), distance).astype(F32)  1.79 us
    select_n x1, other arithmetic, shards(): early = jnp.where(odd, from_mate, total_m)  1.24 us
  transfers between devices with their start and end apart: 5, of which 3 were waited for; matrix products, arithmetic and copies ran while one was open for 2% of the time, Pallas kernels for 32%

profile of v1, /device:TPU:0, one launch (start us, length us, event | category | flops | bytes accessed | tf_op | source)
XLA Modules:
  0.0 58.0 jit_solution(6345252493514209140)
XLA Ops:
  0.0 1.2 %copy-done = bf16[128,4096]{1,0:T(8,128)(2,1)S(1)} copy-done((bf16[128,4096]{1,0:T(8,128)(2,1)S(1)}, bf16[128,4096]{1,0:T(8,128)(2,1)}, u32[]{:S(2)}) %copy-start) | copy-done | bytes 1048600
  1.2 1.2 %copy-done.2 = bf16[128,4096]{1,0:T(8,128)(2,1)S(1)} copy-done((bf16[128,4096]{1,0:T(8,128)(2,1)S(1)}, bf16[128,4096]{1,0:T(8,128)(2,1)}, u32[]{:S(2)}) %copy-start.2) | copy-done | bytes 1048600
  2.5 1.2 %copy-done.4 = bf16[128,4096]{1,0:T(8,128)(2,1)S(1)} copy-done((bf16[128,4096]{1,0:T(8,128)(2,1)S(1)}, bf16[128,4096]{1,0:T(8,128)(2,1)}, u32[]{:S(2)}) %copy-start.4) | copy-done | bytes 1048600
  3.7 0.3 shard_map.91
  4.0 3.0 %collective-permute-start = (bf16[3,8,4096]{2,1,0:T(8,128)(2,1)S(1)}, bf16[3,8,4096]{2,1,0:T(8,128)(2,1)S(1)}, u32[]{:S(2)}, u32[]{:S(2)}) collective-permute-start(bf16[3,8,4096]{2,1,0:T(8,128)(2,1)S(1)} %shard_map.91), channel_id=1, source_target_pairs={{0,2},{2,4},{4,6},{6,8},{8,10},{10,12},{12,14},{14,0},{1,3},{3,5},... | collective-permute-start | bytes 589832 | tf_op jit(solution)/shard_map/ppermute | solution.py:358
  7.0 4.1 %shard_map.93 = (bf16[128,2048]{1,0:T(8,128)(2,1)S(1)}, f32[8,2,16,2048]{3,2,1,0:T(8,128)S(1)}, f32[2,16,2048]{2,1,0:T(8,128)S(1)}, f32[2,16,2048]{2,1,0:T(8,128...) custom-call(bf16[128,4096]{1,0:T(8,128)(2,1)S(1)} %copy-done.1, bf16[128,4096]{1,0:T(8,128)(2,1)S(1)} %copy-done.3, ...), custom_call_target="tpu_custom_call" | custom-call | flops 16777216 | bytes 16777216 | tf_op jit(solution)/shard_map/pallas_call | solution.py:327
  11.1 0.7 %copy-done.25 = f32[2,16,2048]{2,1,0:T(8,128)} copy-done((f32[2,16,2048]{2,1,0:T(8,128)}, f32[2,16,2048]{2,1,0:T(8,128)S(1)}, u32[]{:S(2)}) %copy-start.25) | copy-done | bytes 262168
  11.8 3.1 %collective-permute-done.refs_2_.rim_ref = bf16[3,8,4096]{2,1,0:T(8,128)(2,1)S(1)} collective-permute-done((bf16[3,8,4096]{2,1,0:T(8,128)(2,1)S(1)}, bf16[3,8,4096]{2,1,0:T(8,128)(2,1)S(1)}, u32[]{:S(2)}, u32[]{:S(2)}) %collective-permute-start) | collective-permute-done | bytes 196640 | tf_op jit(solution)/shard_map/ppermute | solution.py:358
  15.0 1.7 %shard_map.94 = (bf16[128,2048]{1,0:T(8,128)(2,1)S(1)}, f32[8,2,16,2048]{3,2,1,0:T(8,128)S(1)}, bf16[2,16,2048]{2,1,0:T(8,128)(2,1)}) custom-call(bf16[128,4096]{1,0:T(8,128)(2,1)S(1)} %copy-done.1, bf16[128,4096]{1,0:T(8,128)(2,1)S(1)} %copy-done.3, ...), custom_call_target="tpu_custom_call", output_to_operand_aliasing={{0}: (7, {}), {1}: (8, {})} | custom-call | flops 2097152 | bytes 2097152 | tf_op jit(solution)/shard_map/pallas_call | solution.py:327
  16.7 1.3 %copy-done.6 = f32[8,2,16,2048]{3,2,1,0:T(8,128)} copy-done((f32[8,2,16,2048]{3,2,1,0:T(8,128)}, f32[8,2,16,2048]{3,2,1,0:T(8,128)S(1)}, u32[]{:S(2)}) %copy-start.6) | copy-done | bytes 2097176
  18.0 0.8 %copy-done.13 = bf16[128,2048]{1,0:T(8,128)(2,1)} copy-done((bf16[128,2048]{1,0:T(8,128)(2,1)}, bf16[128,2048]{1,0:T(8,128)(2,1)S(1)}, u32[]{:S(2)}) %copy-start.13) | copy-done | bytes 524312
  18.8 0.9 %copy-done.16 = f32[16,4096]{1,0:T(8,128)S(1)} copy-done((f32[16,4096]{1,0:T(8,128)S(1)}, f32[16,4096]{1,0:T(8,128)}, u32[]{:S(2)}) %copy-start.16) | copy-done | bytes 262168
  19.8 0.9 %copy-done.18 = f32[16,4096]{1,0:T(8,128)S(1)} copy-done((f32[16,4096]{1,0:T(8,128)S(1)}, f32[16,4096]{1,0:T(8,128)}, u32[]{:S(2)}) %copy-start.18) | copy-done | bytes 262168
  20.7 4.5 %shard_map.92 = (bf16[128,2048]{1,0:T(8,128)(2,1)S(1)}, f32[8,2,16,2048]{3,2,1,0:T(8,128)S(1)}, f32[2,16,2048]{2,1,0:T(8,128)S(1)}, f32[2,16,2048]{2,1,0:T(8,128...) custom-call(bf16[128,4096]{1,0:T(8,128)(2,1)S(1)} %copy-done.1, bf16[128,4096]{1,0:T(8,128)(2,1)S(1)} %copy-done.3, ...), custom_call_target="tpu_custom_call" | custom-call | flops 16777216 | bytes 16777216 | tf_op jit(solution)/shard_map/pallas_call | solution.py:327
  25.3 1.3 %copy-done.11 = f32[8,2,16,2048]{3,2,1,0:T(8,128)} copy-done((f32[8,2,16,2048]{3,2,1,0:T(8,128)}, f32[8,2,16,2048]{3,2,1,0:T(8,128)S(1)}, u32[]{:S(2)}) %copy-start.11) | copy-done | bytes 2097176
  26.6 0.7 %copy-done.27 = f32[2,16,2048]{2,1,0:T(8,128)} copy-done((f32[2,16,2048]{2,1,0:T(8,128)}, f32[2,16,2048]{2,1,0:T(8,128)S(1)}, u32[]{:S(2)}) %copy-start.27) | copy-done | bytes 262168
  27.3 0.7 %copy-done.29 = f32[2,16,2048]{2,1,0:T(8,128)} copy-done((f32[2,16,2048]{2,1,0:T(8,128)}, f32[2,16,2048]{2,1,0:T(8,128)S(1)}, u32[]{:S(2)}) %copy-start.29) | copy-done | bytes 262168
  28.1 1.2 %convert_select_fusion.4 = f32[2,16,2048]{2,1,0:T(8,128)S(1)} fusion(f32[2,16,2048]{2,1,0:T(8,128)S(1)} %get-tuple-element.35, bf16[2,16,2048]{2,1,0:T(8,128)(2,1)} %collective-permute-done.1, pred[]{:T(512)S(6)} %eq.5), kind=kLoop, calls=%fused_computation.4 | loop fusion | flops 131072 | bytes 655361 | tf_op jit(solution)/shard_map/jit(_where)/select_n | solution.py:409
  29.4 1.8 %fusion.3 = (bf16[2,16,2048]{2,1,0:T(8,128)(2,1)}, f32[2,16,2048]{2,1,0:T(8,128)}) fusion(f32[2,16,2048]{2,1,0:T(8,128)S(1)} %get-tuple-element.35, bf16[2,16,2048]{2,1,0:T(8,128)(2,1)} %collective-permute-done.1, pred[]{:T(512)S(6)} %eq.5, f32[1,16,2048]{2,1,0:T(8,128)S(1)} %get-tuple-element.61, f32[1,16,2048]{2,1,0:T(8,128)S(1)} %get-tuple-element.60), kind=kLoop, calls=%fused_computation.23 | loop fusion | flops 327680 | bytes 1048577 | tf_op jit(solution)/shard_map/convert_element_type | solution.py:419
  31.5 3.0 %shard_map.95 = (f32[128,2048]{1,0:T(8,128)S(1)}, f32[128,2048]{1,0:T(8,128)S(1)}, f32[2,16,16,2048]{3,2,1,0:T(8,128)S(1)}) custom-call(bf16[128,4096]{1,0:T(8,128)(2,1)S(1)} %copy-done.5, bf16[3,8,4096]{2,1,0:T(8,128)(2,1)S(1)} %collective-permute-done.refs_2_.rim_ref, bf16[3,7,4096]{2,1,0:T(8,128)(2,1)S(1)} %copy-done.8, f32[1,4096]{1,0:T(1,128)S(1)} %bitcast.1, ...), custom_call_target="tpu_custom_call" | custom-call | flops 8388608 | bytes 8388608 | tf_op jit(solution)/shard_map/pallas_call | solution.py:327
  34.6 1.9 %collective-permute-done.2 = bf16[2,16,2048]{2,1,0:T(8,128)(2,1)} collective-permute-done((bf16[2,16,2048]{2,1,0:T(8,128)(2,1)}, bf16[2,16,2048]{2,1,0:T(8,128)(2,1)}, u32[]{:S(2)}, u32[]{:S(2)}) %collective-permute-start.2) | collective-permute-done | bytes 131104 | tf_op jit(solution)/shard_map/ppermute | solution.py:345
  36.5 0.9 %convert_select_fusion.1 = f32[2,16,2048]{2,1,0:T(8,128)S(1)} fusion(f32[2,16,2048]{2,1,0:T(8,128)S(1)} %copy-done.34, bf16[2,16,2048]{2,1,0:T(8,128)(2,1)} %collective-permute-done.2, pred[]{:T(512)S(6)} %ne.13), kind=kLoop, calls=%fused_computation.1 | loop fusion | flops 131072 | bytes 655361 | tf_op jit(solution)/shard_map/jit(_where)/select_n | solution.py:424
  37.5 0.9 %fusion.2 = bf16[2,16,2048]{2,1,0:T(8,128)(2,1)S(1)} fusion(f32[2,16,2048]{2,1,0:T(8,128)S(1)} %copy-done.34, bf16[2,16,2048]{2,1,0:T(8,128)(2,1)} %collective-permute-done.2, f32[1,16,2048]{2,1,0:T(8,128)S(1)} %multiply_add_fusion.2, f32[1,16,2048]{2,1,0:T(8,128)S(1)} %get-tuple-element.51, pred[]{:T(512)S(6)} %ne.13), kind=kLoop, calls=%fused_computation.7 | loop fusion | flops 327680 | bytes 786433 | tf_op jit(solution)/shard_map/add | solution.py:424
  38.4 1.4 %collective-permute-start.3 = (bf16[2,16,2048]{2,1,0:T(8,128)(2,1)S(1)}, bf16[2,16,2048]{2,1,0:T(8,128)(2,1)S(1)}, u32[]{:S(2)}, u32[]{:S(2)}) collective-permute-start(bf16[2,16,2048]{2,1,0:T(8,128)(2,1)S(1)} %fusion.2), channel_id=1, source_target_pairs={{0,8},{2,10},{4,12},{6,14},{8,0},{10,2},{12,4},{14,6},{1,9},{3,11}... | collective-permute-start | bytes 393224 | tf_op jit(solution)/shard_map/ppermute | solution.py:345
  39.9 3.0 %shard_map.96 = (f32[128,2048]{1,0:T(8,128)S(1)}, f32[128,2048]{1,0:T(8,128)S(1)}, f32[2,16,16,2048]{3,2,1,0:T(8,128)S(1)}) custom-call(bf16[128,4096]{1,0:T(8,128)(2,1)S(1)} %copy-done.5, bf16[3,8,4096]{2,1,0:T(8,128)(2,1)S(1)} %collective-permute-done.refs_2_.rim_ref, bf16[3,7,4096]{2,1,0:T(8,128)(2,1)S(1)} %copy-done.8, f32[1,4096]{1,0:T(1,128)S(1)} %bitcast.2, ...), custom_call_target="tpu_custom_call" | custom-call | flops 8388608 | bytes 8388608 | tf_op jit(solution)/shard_map/pallas_call | solution.py:327
  42.9 2.8 %collective-permute-done.3 = bf16[2,16,2048]{2,1,0:T(8,128)(2,1)S(1)} collective-permute-done((bf16[2,16,2048]{2,1,0:T(8,128)(2,1)S(1)}, bf16[2,16,2048]{2,1,0:T(8,128)(2,1)S(1)}, u32[]{:S(2)}, u32[]{:S(2)}) %collective-permute-start.3) | collective-permute-done | bytes 131104 | tf_op jit(solution)/shard_map/ppermute | solution.py:345
  45.8 1.1 %fusion.1 = f32[2,16,2048]{2,1,0:T(8,128)S(1)} fusion(bf16[2,16,2048]{2,1,0:T(8,128)(2,1)} %collective-permute-done.2, f32[1,16,2048]{2,1,0:T(8,128)S(1)} %get-tuple-element.59, f32[1,16,2048]{2,1,0:T(8,128)S(1)} %get-tuple-element.58, pred[]{:T(512)S(6)} %ne.14, pred[]{:T(512)S(6)} %ne.13), kind=kLoop, calls=%fused_computation.6 | loop fusion | flops 327680 | bytes 655362 | tf_op jit(solution)/shard_map/add | solution.py:422
  47.0 1.0 %select_convert_fusion = bf16[2,16,2048]{2,1,0:T(8,128)(2,1)S(1)} fusion(pred[]{:T(512)S(6)} %eq.5, f32[2,16,2048]{2,1,0:T(8,128)S(1)} %copy-done.33, f32[1,16,2048]{2,1,0:T(8,128)S(1)} %get-tuple-element.57, f32[1,16,2048]{2,1,0:T(8,128)S(1)} %get-tuple-element.56, f32[1,16,2048]{2,1,0:T(8,128)S(1)} %get-tuple-element.59, ...), kind=kLoop, calls=%fused_computation.11 | loop fusion | flops 524288 | bytes 1048579 | tf_op jit(solution)/shard_map/convert_element_type | solution.py:436
  47.9 1.8 %collective-permute-start.4 = (bf16[2,16,2048]{2,1,0:T(8,128)(2,1)S(1)}, bf16[2,16,2048]{2,1,0:T(8,128)(2,1)S(1)}, u32[]{:S(2)}, u32[]{:S(2)}) collective-permute-start(bf16[2,16,2048]{2,1,0:T(8,128)(2,1)S(1)} %select_convert_fusion), channel_id=1, source_target_pairs={{0,2},{2,0},{4,6},{6,4},{8,10},{10,8},{12,14},{14,12},{1,3},{3,1},... | collective-permute-start | bytes 393224 | tf_op jit(solution)/shard_map/ppermute | solution.py:345
  49.7 1.0 %broadcast_select_fusion.enter_ref = f32[2,16,2048]{2,1,0:T(8,128)S(1)} fusion(pred[]{:T(512)S(6)} %eq.5, f32[2,16,2048]{2,1,0:T(8,128)S(1)} %copy-done.33, f32[1,16,2048]{2,1,0:T(8,128)S(1)} %get-tuple-element.57, f32[1,16,2048]{2,1,0:T(8,128)S(1)} %get-tuple-element.56, f32[1,16,2048]{2,1,0:T(8,128)S(1)} %get-tuple-element.59, ...), kind=kLoop, calls=%fused_computation.22 | loop fusion | flops 524288 | bytes 1179651 | tf_op jit(solution)/shard_map/jit(_where)/select_n | solution.py:437
  50.7 3.6 %shard_map.97.rest_0_ = bf16[128,4096]{1,0:T(8,128)(2,1)} custom-call(f32[2,16,2048]{2,1,0:T(8,128)S(1)} %broadcast_select_fusion.enter_ref, f32[8,2,16,2048]{3,2,1,0:T(8,128)S(1)} %copy-done.12, f32[2,16,2048]{2,1,0:T(8,128)S(1)} %copy-done.28, f32[2,16,16,2048]{3,2,1,0:T(8,128)S(1)} %get-tuple-element.48.pow_ref, ...), custom_call_target="tpu_custom_call" | custom-call | flops 8388608 | bytes 8388608 | tf_op jit(solution)/shard_map/pallas_call | solution.py:327
  54.4 3.6 %shard_map.98 = bf16[128,4096]{1,0:T(8,128)(2,1)} custom-call(bf16[2,16,2048]{2,1,0:T(8,128)(2,1)S(1)} %collective-permute-done.4.enter_ref, f32[8,2,16,2048]{3,2,1,0:T(8,128)S(1)} %copy-done.7, f32[2,16,2048]{2,1,0:T(8,128)S(1)} %copy-done.26, f32[2,16,16,2048]{3,2,1,0:T(8,128)S(1)} %get-tuple-element.41.pow_ref, ...), custom_call_target="tpu_custom_call", output_to_operand_aliasing={{}: (6, {})} | custom-call | flops 8388608 | bytes 8388608 | tf_op jit(solution)/shard_map/pallas_call | solution.py:327
  (72 shorter events, 0.6 us)
Async XLA Ops:
  3.7 3.3 %copy-start.1 = (bf16[128,4096]{1,0:T(8,128)(2,1)S(1)}, bf16[128,4096]{1,0:T(8,128)(2,1)}, u32[]{:S(2)}) copy-start(bf16[128,4096]{1,0:T(8,128)(2,1)} %k_ref.1) | copy-start | bytes 3145732
  3.7 3.3 %copy-start.3 = (bf16[128,4096]{1,0:T(8,128)(2,1)S(1)}, bf16[128,4096]{1,0:T(8,128)(2,1)}, u32[]{:S(2)}) copy-start(bf16[128,4096]{1,0:T(8,128)(2,1)} %v_ref.1) | copy-start | bytes 3145732
  3.7 3.3 %copy-start.8 = (bf16[3,7,4096]{2,1,0:T(8,128)(2,1)S(1)}, bf16[3,7,4096]{2,1,0:T(8,128)(2,1)}, u32[]{:S(2)}) copy-start(bf16[3,7,4096]{2,1,0:T(8,128)(2,1)} %taps_ref.5) | copy-start | bytes 516100
  3.7 3.3 %copy-start.15 = (f32[16,4096]{1,0:T(8,128)S(1)}, f32[16,4096]{1,0:T(8,128)}, u32[]{:S(2)}) copy-start(f32[16,4096]{1,0:T(8,128)} %refs_3_.3) | copy-start | bytes 786436
  3.7 3.3 %copy-start.17 = (f32[16,4096]{1,0:T(8,128)S(1)}, f32[16,4096]{1,0:T(8,128)}, u32[]{:S(2)}) copy-start(f32[16,4096]{1,0:T(8,128)} %refs_4_.3) | copy-start | bytes 786436
  4.0 11.0 %collective-permute-start = (bf16[3,8,4096]{2,1,0:T(8,128)(2,1)S(1)}, bf16[3,8,4096]{2,1,0:T(8,128)(2,1)S(1)}, u32[]{:S(2)}, u32[]{:S(2)}) collective-permute-start(bf16[3,8,4096]{2,1,0:T(8,128)(2,1)S(1)} %shard_map.91), channel_id=1, source_target_pairs={{0,2},{2,4},{4,6},{6,8},{8,10},{10,12},{12,14},{14,0},{1,3},{3,5},... | collective-permute-start | bytes 589832 | tf_op jit(solution)/shard_map/ppermute | solution.py:358
  11.8 4.9 %copy-start.19 = (f32[2,16,2048]{2,1,0:T(8,128)}, f32[2,16,2048]{2,1,0:T(8,128)S(1)}, u32[]{:S(2)}) copy-start(f32[2,16,2048]{2,1,0:T(8,128)S(1)} %get-tuple-element.29.lam_ref) | copy-start | bytes 786436
  16.7 1.3 %copy-start.6 = (f32[8,2,16,2048]{3,2,1,0:T(8,128)}, f32[8,2,16,2048]{3,2,1,0:T(8,128)S(1)}, u32[]{:S(2)}) copy-start(f32[8,2,16,2048]{3,2,1,0:T(8,128)S(1)} %get-tuple-element.38.chunk_ref) | copy-start | bytes 6291460
  18.8 9.2 %collective-permute-start.1 = (bf16[2,16,2048]{2,1,0:T(8,128)(2,1)}, bf16[2,16,2048]{2,1,0:T(8,128)(2,1)}, u32[]{:S(2)}, u32[]{:S(2)}) collective-permute-start(bf16[2,16,2048]{2,1,0:T(8,128)(2,1)} %get-tuple-element.34), channel_id=1, source_target_pairs={{0,2},{2,0},{4,6},{6,4},{8,10},{10,8},{12,14},{14,12},{1,3},{3,1},... | collective-permute-start | bytes 393224 | tf_op jit(solution)/shard_map/ppermute | solution.py:345
  20.7 10.7 %copy-start.5 = (bf16[128,4096]{1,0:T(8,128)(2,1)S(1)}, bf16[128,4096]{1,0:T(8,128)(2,1)}, u32[]{:S(2)}) copy-start(bf16[128,4096]{1,0:T(8,128)(2,1)} %q_ref.3) | copy-start | bytes 3145732
  20.7 10.7 %copy-start.31 = (f32[4096]{0:T(1024)S(1)}, f32[4096]{0:T(1024)}, u32[]{:S(2)}) copy-start(f32[4096]{0:T(1024)} %param.17) | copy-start | bytes 49156
  25.3 1.3 %copy-start.11 = (f32[8,2,16,2048]{3,2,1,0:T(8,128)}, f32[8,2,16,2048]{3,2,1,0:T(8,128)S(1)}, u32[]{:S(2)}) copy-start(f32[8,2,16,2048]{3,2,1,0:T(8,128)S(1)} %get-tuple-element.44.chunk_ref) | copy-start | bytes 6291460
  28.0 1.3 %copy-start.9 = (f32[2,16,2048]{2,1,0:T(8,128)}, f32[2,16,2048]{2,1,0:T(8,128)S(1)}, u32[]{:S(2)}) copy-start(f32[2,16,2048]{2,1,0:T(8,128)S(1)} %get-tuple-element.28) | copy-start | bytes 786436
  28.0 1.4 %copy-start.23 = (bf16[128,2048]{1,0:T(8,128)(2,1)}, bf16[128,2048]{1,0:T(8,128)(2,1)S(1)}, u32[]{:S(2)}) copy-start(bf16[128,2048]{1,0:T(8,128)(2,1)S(1)} %get-tuple-element.47.gated_ref) | copy-start | bytes 1572868
  28.0 3.4 %copy-start.14 = (bf16[128,2048]{1,0:T(8,128)(2,1)S(1)}, bf16[128,2048]{1,0:T(8,128)(2,1)}, u32[]{:S(2)}) copy-start(bf16[128,2048]{1,0:T(8,128)(2,1)} %copy-done.13) | copy-start | bytes 1572868
  28.0 3.4 %copy-start.20 = (f32[2,16,2048]{2,1,0:T(8,128)S(1)}, f32[2,16,2048]{2,1,0:T(8,128)}, u32[]{:S(2)}) copy-start(f32[2,16,2048]{2,1,0:T(8,128)} %copy-done.19) | copy-start | bytes 786436
  28.0 3.4 %copy-start.21 = (f32[16,4096]{1,0:T(8,128)S(1)}, f32[16,4096]{1,0:T(8,128)}, u32[]{:S(2)}) copy-start(f32[16,4096]{1,0:T(8,128)} %res_re_ref.3) | copy-start | bytes 786436
  28.1 3.4 %copy-start.22 = (f32[16,4096]{1,0:T(8,128)S(1)}, f32[16,4096]{1,0:T(8,128)}, u32[]{:S(2)}) copy-start(f32[16,4096]{1,0:T(8,128)} %res_im_ref.3) | copy-start | bytes 786436
  29.3 5.2 %copy-start.32 = (f32[2,16,2048]{2,1,0:T(8,128)}, f32[2,16,2048]{2,1,0:T(8,128)S(1)}, u32[]{:S(2)}) copy-start(f32[2,16,2048]{2,1,0:T(8,128)S(1)} %convert_select_fusion.4) | copy-start | bytes 786436
  29.4 8.0 %copy-start.10 = (f32[2,16,2048]{2,1,0:T(8,128)S(1)}, f32[2,16,2048]{2,1,0:T(8,128)}, u32[]{:S(2)}) copy-start(f32[2,16,2048]{2,1,0:T(8,128)} %copy-done.9) | copy-start | bytes 786436
  31.2 5.3 %collective-permute-start.2 = (bf16[2,16,2048]{2,1,0:T(8,128)(2,1)}, bf16[2,16,2048]{2,1,0:T(8,128)(2,1)}, u32[]{:S(2)}, u32[]{:S(2)}) collective-permute-start(bf16[2,16,2048]{2,1,0:T(8,128)(2,1)} %get-tuple-element.54), channel_id=1, source_target_pairs={{0,4},{2,6},{4,0},{6,2},{8,12},{10,14},{12,8},{14,10},{1,5},{3,7},... | collective-permute-start | bytes 393224 | tf_op jit(solution)/shard_map/ppermute | solution.py:345
  31.5 5.0 %copy-start.34 = (f32[2,16,2048]{2,1,0:T(8,128)S(1)}, f32[2,16,2048]{2,1,0:T(8,128)}, u32[]{:S(2)}) copy-start(f32[2,16,2048]{2,1,0:T(8,128)} %get-tuple-element.55) | copy-start | bytes 786436
  34.6 5.2 %copy-start.35 = (f32[2,16,2048]{2,1,0:T(8,128)S(1)}, f32[2,16,2048]{2,1,0:T(8,128)}, u32[]{:S(2)}) copy-start(f32[2,16,2048]{2,1,0:T(8,128)} %constant.26.clone.1) | copy-start | bytes 786436
  34.6 5.3 %copy-start.24 = (bf16[128,2048]{1,0:T(8,128)(2,1)S(1)}, bf16[128,2048]{1,0:T(8,128)(2,1)}, u32[]{:S(2)}) copy-start(bf16[128,2048]{1,0:T(8,128)(2,1)} %copy-done.23) | copy-start | bytes 1572868
  34.6 5.3 %copy-start.30 = (f32[2,16,2048]{2,1,0:T(8,128)S(1)}, f32[2,16,2048]{2,1,0:T(8,128)}, u32[]{:S(2)}) copy-start(f32[2,16,2048]{2,1,0:T(8,128)} %copy-done.29) | copy-start | bytes 786436
  38.4 7.3 %collective-permute-start.3 = (bf16[2,16,2048]{2,1,0:T(8,128)(2,1)S(1)}, bf16[2,16,2048]{2,1,0:T(8,128)(2,1)S(1)}, u32[]{:S(2)}, u32[]{:S(2)}) collective-permute-start(bf16[2,16,2048]{2,1,0:T(8,128)(2,1)S(1)} %fusion.2), channel_id=1, source_target_pairs={{0,8},{2,10},{4,12},{6,14},{8,0},{10,2},{12,4},{14,6},{1,9},{3,11}... | collective-permute-start | bytes 393224 | tf_op jit(solution)/shard_map/ppermute | solution.py:345
  39.9 7.1 %copy-start.33 = (f32[2,16,2048]{2,1,0:T(8,128)S(1)}, f32[2,16,2048]{2,1,0:T(8,128)}, u32[]{:S(2)}) copy-start(f32[2,16,2048]{2,1,0:T(8,128)} %copy-done.32) | copy-start | bytes 786436
  45.7 5.0 %copy-start.12 = (f32[8,2,16,2048]{3,2,1,0:T(8,128)S(1)}, f32[8,2,16,2048]{3,2,1,0:T(8,128)}, u32[]{:S(2)}) copy-start(f32[8,2,16,2048]{3,2,1,0:T(8,128)} %copy-done.11) | copy-start | bytes 6291460
  45.8 5.0 %copy-start.28 = (f32[2,16,2048]{2,1,0:T(8,128)S(1)}, f32[2,16,2048]{2,1,0:T(8,128)}, u32[]{:S(2)}) copy-start(f32[2,16,2048]{2,1,0:T(8,128)} %copy-done.27) | copy-start | bytes 786436
  47.9 6.5 %collective-permute-start.4 = (bf16[2,16,2048]{2,1,0:T(8,128)(2,1)S(1)}, bf16[2,16,2048]{2,1,0:T(8,128)(2,1)S(1)}, u32[]{:S(2)}, u32[]{:S(2)}) collective-permute-start(bf16[2,16,2048]{2,1,0:T(8,128)(2,1)S(1)} %select_convert_fusion), channel_id=1, source_target_pairs={{0,2},{2,0},{4,6},{6,4},{8,10},{10,8},{12,14},{14,12},{1,3},{3,1},... | collective-permute-start | bytes 393224 | tf_op jit(solution)/shard_map/ppermute | solution.py:345
  50.7 3.7 %copy-start.7 = (f32[8,2,16,2048]{3,2,1,0:T(8,128)S(1)}, f32[8,2,16,2048]{3,2,1,0:T(8,128)}, u32[]{:S(2)}) copy-start(f32[8,2,16,2048]{3,2,1,0:T(8,128)} %copy-done.6) | copy-start | bytes 6291460
  50.7 3.7 %copy-start.26 = (f32[2,16,2048]{2,1,0:T(8,128)S(1)}, f32[2,16,2048]{2,1,0:T(8,128)}, u32[]{:S(2)}) copy-start(f32[2,16,2048]{2,1,0:T(8,128)} %copy-done.25) | copy-start | bytes 786436
  (9 other events, 8.5 us)

commit v2 on v1

--- a/solution.py
+++ b/solution.py
@@ -182,11 +182,12 @@
     over_tiles(width, base, tile)
 
 
-def local_kernel(mine, q_ref, rim_ref, taps_ref, gain_ref, res_re_ref, res_im_ref, lam_ref, gated_ref,
+def local_kernel(mine, after_ref, q_ref, rim_ref, taps_ref, gain_ref, res_re_ref, res_im_ref, lam_ref, gated_ref,
                  query_ref, local_ref, pow_ref, pad_q, gate, tap_q, table_re, table_im, line, mix):
     length = q_ref.shape[0]
     width = gated_ref.shape[1]
     modes = lam_ref.shape[1]
+    del after_ref
     first, base = half_start(width, mine)
     chunks = length // CHUNK
     side = ROWS // 2
@@ -293,8 +294,74 @@
         copy(piece).wait()
 
 
+def is_odd(distance):
+    return lax.rem(lax.div(lax.axis_index("seq"), distance), 2) == 1
+
+
+def pick(flag, a, b):
+    return jnp.where(flag, a[0], b[0]), jnp.where(flag, a[1], b[1])
+
+
+def each_tile(width, body):
+    def visit(i, carry):
+        body(aligned(i * LANES))
+        return carry
+
+    lax.fori_loop(0, width // LANES, visit, 0)
+
+
+def pair_kernel(mate_ref, total_ref, span_ref, sent_ref, block_ref, early_ref):
+    odd = is_odd(1)
+
+    def tile(lanes):
+        mate, own = get(mate_ref, lanes), get(total_ref, lanes)
+        early, late = pick(odd, mate, own), pick(odd, own, mate)
+        block = add(cmul(*get(span_ref, lanes), *early), late)
+        put(early_ref, lanes, early)
+        put(block_ref, lanes, block)
+        put(sent_ref, lanes, block)
+
+    each_tile(total_ref.shape[-1], tile)
+
+
+def stage_kernel(distance, last, *refs):
+    refs = list(refs)
+    arrived_ref, span_ref = refs[:2]
+    refs = refs[3:]
+    block_ref = refs.pop(0)
+    enter_ref = refs.pop(0) if distance > 2 else None
+    early_ref = refs.pop(0) if last else None
+    upper = is_odd(distance)
+    odd = is_odd(1)
+
+    def tile(lanes):
+        arrived, span = get(arrived_ref, lanes), get(span_ref, lanes)
+        moved = arrived
+        power = cmul(*span, *span)
+        bit = 2
+        while bit < distance:
+            moved = pick(is_odd(bit), cmul(*power, *moved), moved)
+            power = cmul(*power, *power)
+            bit *= 2
+        enter = jnp.where(upper, moved[0], 0.0), jnp.where(upper, moved[1], 0.0)
+        if enter_ref is not None:
+            enter = add(enter, get(enter_ref, lanes))
+        if last:
+            past = add(cmul(*span, *enter), get(early_ref, lanes))
+            put(refs[0], lanes, pick(odd, enter, past))
+            put(refs[1], lanes, pick(odd, past, enter))
+        else:
+            block = get(block_ref, lanes)
+            block = add(cmul(*power, *pick(upper, arrived, block)), pick(upper, block, arrived))
+            put(refs[0], lanes, block)
+            put(refs[1], lanes, block)
+            put(refs[2], lanes, enter)
+
+    each_tile(span_ref.shape[-1], tile)
+
+
 def tails_kernel(*refs):
-    count = (len(refs) - 2) // 1
+    count = len(refs) - 2
     sources, out_ref, sems = refs[:count], refs[count], refs[count + 1]
     copies = [
         pltpu.make_async_copy(ref.at[pl.ds(ref.shape[0] - ROWS, ROWS), :], out_ref.at[n], sems.at[n])
@@ -315,8 +382,6 @@
     half = channels // 2
     chunks = length // CHUNK
     axis_size = lax.axis_size("seq")
-    index = lax.axis_index("seq")
-    odd = index % 2 == 1
     inside = pl.BlockSpec(memory_space=pltpu.VMEM)
     outside = pl.BlockSpec(memory_space=pl.ANY)
 
@@ -344,15 +409,12 @@
     def swap(block, distance):
         return lax.ppermute(block, "seq", [(i, i ^ distance) for i in range(axis_size)])
 
-    def times(a, b):
-        return jnp.stack(cmul(a[0], a[1], b[0], b[1]))
-
     gates = pltpu.VMEM((length, half), BF16)
     sums = pltpu.VMEM((chunks, 2, modes, half), F32)
     pads = [rows(length + ROWS), rows(length + ROWS), rows(length), rows(ROWS), rows(ROWS)]
 
     tails = call(
-        tails_kernel, [q_proj, k_proj, v_proj], pltpu.VMEM((branches, ROWS, channels), q_proj.dtype),
+        tails_kernel, [pltpu.with_memory_space_constraint(x, pltpu.HBM) for x in (q_proj, k_proj, v_proj)], pltpu.VMEM((branches, ROWS, channels), q_proj.dtype),
         [pltpu.SemaphoreType.DMA((branches,))], 1 << 16, in_specs=[outside] * branches,
     )
     rims = lax.ppermute(tails, "seq", [(i, (i + 1) % axis_size) for i in range(axis_size)])
@@ -378,10 +440,10 @@
         [gates, sums, modal(), modal(), modal(), modal()], pads, 16 << 20,
     )
 
-    def local(mine, lam, gated):
+    def local(mine, lam, gated, after):
         return call(
             functools.partial(local_kernel, mine),
-            [q, near(rims), taps, gain, res_re, res_im, near(lam), near(gated)],
+            [near(after), q, near(rims), taps, gain, res_re, res_im, near(lam), near(gated)],
             [pltpu.VMEM((length, half), F32), pltpu.VMEM((length, half), F32), pltpu.VMEM((2, modes, CHUNK, half), F32)],
             [rows(length + ROWS), rows(2 * length), rows(ROWS), rows(CHUNK * modes), rows(CHUNK * modes),
              rows(6 * modes), rows(8 * modes)],
@@ -405,36 +467,31 @@
             8 << 20, aliases, specs, outside,
         )
 
-    from_mate = from_mate.astype(F32)
-    early = jnp.where(odd, from_mate, total_m)
-    late = jnp.where(odd, total_m, from_mate)
-    block = times(span, early) + late
-    made_o = local(False, lam_o, gated_o)
-    made_m = None
-    power = times(span, span)
-    enter = jnp.zeros_like(block)
-    decay = None
+    sent, block, early = call(
+        pair_kernel, [near(from_mate), near(total_m), near(span)], [modal(BF16), modal(), modal()], [], 1 << 18,
+    )
+    makers = [functools.partial(local, False, lam_o, gated_o), functools.partial(local, True, lam_m, gated_m)]
+    made = []
+    enter = []
     distance = 2
     while distance < axis_size:
-        arrived = swap(block.astype(BF16), distance).astype(F32)
-        upper = (index & distance) != 0
-        moved = arrived if decay is None else times(decay, arrived)
-        enter = enter + jnp.where(upper, moved, 0.0)
-        if 2 * distance < axis_size:
-            block = times(power, jnp.where(upper, arrived, block)) + jnp.where(upper, block, arrived)
-            one = jnp.stack([jnp.ones_like(power[0]), jnp.zeros_like(power[0])])
-            grown = jnp.where(upper, power, one)
-            decay = grown if decay is None else times(decay, grown)
-            power = times(power, power)
-            if made_m is None:
-                gated_m, block = lax.optimization_barrier((gated_m, block))
-                made_m = local(True, lam_m, gated_m)
+        last = 2 * distance >= axis_size
+        arrived = swap(sent, distance)
+        while makers and (last or len(made) * 2 < distance):
+            made.append(makers.pop(0)(block))
+        args = [arrived, span, made[-1][0], block] + enter + ([early] if last else [])
+        results = call(
+            functools.partial(stage_kernel, distance, last), [near(array) for array in args],
+            [modal(BF16), modal()] if last else [modal(BF16), modal(), modal()], [], 1 << 18,
+        )
+        if last:
+            handed, mine = results
+        else:
+            sent, block, entered = results
+            enter = [entered]
         distance *= 2
-    if made_m is None:
-        made_m = local(True, lam_m, gated_m)
-    past = times(span, enter) + early
-    handed = swap(jnp.where(odd, enter, past).astype(BF16), 1)
-    mine = jnp.where(odd, past, enter)
+    made_o, made_m = made
+    handed = swap(handed, 1)
     out = finish(True, mine, chunk_m, step_m, made_m)
     return finish(False, handed, chunk_o, step_o, made_o, out)
 

time: 58.5 us -> 40.1 us (0.69)
  local copies, waits for them, and re-layouts: 11.3 us -> 0.04 us
  other arithmetic: 8.15 us -> 0 us
  waiting for transfers between devices: 7.79 us -> 9.06 us
  Pallas kernels: 24 us -> 24.8 us
    unnamed x72 -> x18, local copies, waits for them, and re-layouts: 11.3 us -> 0.04 us
    select_n x4 -> x0, other arithmetic: 3.18 us -> none  [the longest x1 1.24 us: shards(): early = jnp.where(odd, from_mate, total_m)]
    convert_element_type x3 -> x0, other arithmetic: 2.76 us -> none  [the longest x2 1.79 us: shards(): arrived = swap(block.astype(BF16), distance).astype(F32)]
    add x3 -> x0, other arithmetic: 2.07 us -> none  [the longest x1 1.09 us: shards(): enter = enter + jnp.where(upper, moved, 0.0)]
    pallas_call x8 -> x11, Pallas kernels: 24 us -> 24.8 us  [call(): pl.pallas_call(kernel, out_shape=outs, in_specs=in_specs or [inside] * le...]
    ppermute x1, waiting for transfers between devices: 3.11 us -> 3.85 us  [shards(): lax.ppermute(tails, 'seq', [(i, (i + 1) % axis_size) for i in range(axis_...]
    ppermute x4, starting transfers between devices: 3.44 us -> 2.85 us  [swap(): lax.ppermute(block, 'seq', [(i, i ^ distance) for i in range(axis_size)])]
  transfers between devices with their start and end apart: 5 -> 5, of which waited for: 3 -> 4; matrix products, arithmetic and copies ran while one was open for 2% -> 0% of each run, Pallas kernels for 32% -> 46%
where the time goes in v2:
time: 40.1 us; the launch traced here: 40 us
  Pallas kernels  24.8 us (62%)
  waiting for transfers between devices  9.06 us (23%)
  starting transfers between devices  5.89 us (15%)
    pallas_call x11, Pallas kernels, call(): pl.pallas_call(kernel, out_shape=outs, in_specs=in_specs or [inside] * le...  24.8 us
    ppermute x4, waiting for transfers between devices, swap(): lax.ppermute(block, 'seq', [(i, i ^ distance) for i in range(axis_size)])  5.21 us
    ppermute x1, waiting for transfers between devices, shards(): lax.ppermute(tails, 'seq', [(i, (i + 1) % axis_size) for i in range(axis_...  3.85 us
    ppermute x1, starting transfers between devices, shards(): lax.ppermute(tails, 'seq', [(i, (i + 1) % axis_size) for i in range(axis_...  3.03 us
    ppermute x4, starting transfers between devices, swap(): lax.ppermute(block, 'seq', [(i, i ^ distance) for i in range(axis_size)])  2.85 us
  transfers between devices with their start and end apart: 5, of which 4 were waited for; matrix products, arithmetic and copies ran while one was open for 0% of the time, Pallas kernels for 46%

profile of v2, /device:TPU:0, one launch (start us, length us, event | category | flops | bytes accessed | tf_op | source)
XLA Modules:
  0.0 40.0 jit_solution(7641871152835381458)
XLA Ops:
  0.0 1.1 %shard_map.91 = bf16[3,8,4096]{2,1,0:T(8,128)(2,1)S(1)} custom-call(bf16[128,4096]{1,0:T(8,128)(2,1)} %q_ref.3, bf16[128,4096]{1,0:T(8,128)(2,1)} %refs_0_.5, bf16[128,4096]{1,0:T(8,128)(2,1)} %refs_1_.5), custom_call_target="tpu_custom_call" | custom-call | flops 65536 | bytes 65536 | tf_op jit(solution)/shard_map/pallas_call | solution.py:392
  1.1 3.0 %collective-permute-start = (bf16[3,8,4096]{2,1,0:T(8,128)(2,1)S(1)}, bf16[3,8,4096]{2,1,0:T(8,128)(2,1)S(1)}, u32[]{:S(2)}, u32[]{:S(2)}) collective-permute-start(bf16[3,8,4096]{2,1,0:T(8,128)(2,1)S(1)} %shard_map.91), channel_id=1, source_target_pairs={{0,2},{2,4},{4,6},{6,8},{8,10},{10,12},{12,14},{14,0},{1,3},{3,5},... | collective-permute-start | bytes 589832 | tf_op jit(solution)/shard_map/ppermute | solution.py:420
  4.1 0.0 copy-done.1
  4.1 0.0 copy-done
  4.1 0.0 copy-done.3
  4.1 0.0 copy-done.7
  4.2 0.0 copy-done.6
  4.2 4.1 %shard_map.92 = (bf16[128,2048]{1,0:T(8,128)(2,1)S(1)}, f32[8,2,16,2048]{3,2,1,0:T(8,128)S(1)}, f32[2,16,2048]{2,1,0:T(8,128)S(1)}, f32[2,16,2048]{2,1,0:T(8,128...) custom-call(bf16[128,4096]{1,0:T(8,128)(2,1)S(1)} %copy-done, bf16[128,4096]{1,0:T(8,128)(2,1)S(1)} %copy-done.1, ...), custom_call_target="tpu_custom_call" | custom-call | flops 16777216 | bytes 16777216 | tf_op jit(solution)/shard_map/pallas_call | solution.py:392
  8.2 3.9 %collective-permute-done.rim_ref.refs_2_ = bf16[3,8,4096]{2,1,0:T(8,128)(2,1)S(1)} collective-permute-done((bf16[3,8,4096]{2,1,0:T(8,128)(2,1)S(1)}, bf16[3,8,4096]{2,1,0:T(8,128)(2,1)S(1)}, u32[]{:S(2)}, u32[]{:S(2)}) %collective-permute-start) | collective-permute-done | bytes 196640 | tf_op jit(solution)/shard_map/ppermute | solution.py:420
  12.1 1.1 %shard_map.93 = (bf16[128,2048]{1,0:T(8,128)(2,1)S(1)}, f32[8,2,16,2048]{3,2,1,0:T(8,128)S(1)}, bf16[2,16,2048]{2,1,0:T(8,128)(2,1)S(1)}) custom-call(bf16[128,4096]{1,0:T(8,128)(2,1)S(1)} %copy-done, bf16[128,4096]{1,0:T(8,128)(2,1)S(1)} %copy-done.1, ...), custom_call_target="tpu_custom_call", output_to_operand_aliasing={{0}: (7, {}), {1}: (8, {})} | custom-call | flops 2097152 | bytes 2097152 | tf_op jit(solution)/shard_map/pallas_call | solution.py:392
  13.2 0.0 copy-start.2
  13.2 0.0 copy-start.4
  13.2 0.0 copy-start.5
  13.2 0.0 copy-start.8
  13.2 0.1 collective-permute-start.1
  13.3 4.5 %shard_map.94 = (bf16[128,2048]{1,0:T(8,128)(2,1)S(1)}, f32[8,2,16,2048]{3,2,1,0:T(8,128)S(1)}, f32[2,16,2048]{2,1,0:T(8,128)S(1)}, f32[2,16,2048]{2,1,0:T(8,128...) custom-call(bf16[128,4096]{1,0:T(8,128)(2,1)S(1)} %copy-done, bf16[128,4096]{1,0:T(8,128)(2,1)S(1)} %copy-done.1, ...), custom_call_target="tpu_custom_call" | custom-call | flops 16777216 | bytes 16777216 | tf_op jit(solution)/shard_map/pallas_call | solution.py:392
  17.8 0.4 %collective-permute-done.1.mate_ref = bf16[2,16,2048]{2,1,0:T(8,128)(2,1)S(1)} collective-permute-done((bf16[2,16,2048]{2,1,0:T(8,128)(2,1)S(1)}, bf16[2,16,2048]{2,1,0:T(8,128)(2,1)S(1)}, u32[]{:S(2)}, u32[]{:S(2)}) %collective-permute-start.1) | collective-permute-done | bytes 131104 | tf_op jit(solution)/shard_map/ppermute | solution.py:410
  18.3 0.2 shard_map.95
  18.5 0.1 collective-permute-start.2
  18.6 0.0 copy-done.2
  18.6 0.0 copy-done.4
  18.6 3.0 %shard_map.96 = (f32[128,2048]{1,0:T(8,128)S(1)}, f32[128,2048]{1,0:T(8,128)S(1)}, f32[2,16,16,2048]{3,2,1,0:T(8,128)S(1)}) custom-call(f32[2,16,2048]{2,1,0:T(8,128)S(1)} %get-tuple-element.43.after_ref.refs_3_, bf16[128,4096]{1,0:T(8,128)(2,1)S(1)} %copy-done.2, bf16[3,8,4096]{2,1,0:T(8,128)(2,1)S(1)} %collective-permute-done.rim_ref.refs_2_, ...), custom_call_target="tpu_custom_call" | custom-call | flops 8388608 | bytes 8388608 | tf_op jit(solution)/shard_map/pallas_call | solution.py:392
  21.7 1.9 %collective-permute-done.2.refs_0_ = bf16[2,16,2048]{2,1,0:T(8,128)(2,1)S(1)} collective-permute-done((bf16[2,16,2048]{2,1,0:T(8,128)(2,1)S(1)}, bf16[2,16,2048]{2,1,0:T(8,128)(2,1)S(1)}, u32[]{:S(2)}, u32[]{:S(2)}) %collective-permute-start.2) | collective-permute-done | bytes 131104 | tf_op jit(solution)/shard_map/ppermute | solution.py:410
  23.5 0.2 shard_map.97
  23.7 1.0 %collective-permute-start.3 = (bf16[2,16,2048]{2,1,0:T(8,128)(2,1)S(1)}, bf16[2,16,2048]{2,1,0:T(8,128)(2,1)S(1)}, u32[]{:S(2)}, u32[]{:S(2)}) collective-permute-start(bf16[2,16,2048]{2,1,0:T(8,128)(2,1)S(1)} %get-tuple-element.46), channel_id=1, source_target_pairs={{0,8},{2,10},{4,12},{6,14},{8,0},{10,2},{12,4},{14,6},{1,9},{3,11}... | collective-permute-start | bytes 393224 | tf_op jit(solution)/shard_map/ppermute | solution.py:410
  24.7 3.0 %shard_map.98 = (f32[128,2048]{1,0:T(8,128)S(1)}, f32[128,2048]{1,0:T(8,128)S(1)}, f32[2,16,16,2048]{3,2,1,0:T(8,128)S(1)}) custom-call(f32[2,16,2048]{2,1,0:T(8,128)S(1)} %get-tuple-element.47.after_ref.refs_3_, bf16[128,4096]{1,0:T(8,128)(2,1)S(1)} %copy-done.2, bf16[3,8,4096]{2,1,0:T(8,128)(2,1)S(1)} %collective-permute-done.rim_ref.refs_2_, ...), custom_call_target="tpu_custom_call" | custom-call | flops 8388608 | bytes 8388608 | tf_op jit(solution)/shard_map/pallas_call | solution.py:392
  27.7 2.9 %collective-permute-done.3.refs_0_ = bf16[2,16,2048]{2,1,0:T(8,128)(2,1)S(1)} collective-permute-done((bf16[2,16,2048]{2,1,0:T(8,128)(2,1)S(1)}, bf16[2,16,2048]{2,1,0:T(8,128)(2,1)S(1)}, u32[]{:S(2)}, u32[]{:S(2)}) %collective-permute-start.3) | collective-permute-done | bytes 131104 | tf_op jit(solution)/shard_map/ppermute | solution.py:410
  30.7 0.3 shard_map.99
  31.0 1.8 %collective-permute-start.4 = (bf16[2,16,2048]{2,1,0:T(8,128)(2,1)S(1)}, bf16[2,16,2048]{2,1,0:T(8,128)(2,1)S(1)}, u32[]{:S(2)}, u32[]{:S(2)}) collective-permute-start(bf16[2,16,2048]{2,1,0:T(8,128)(2,1)S(1)} %get-tuple-element.53), channel_id=1, source_target_pairs={{0,2},{2,0},{4,6},{6,4},{8,10},{10,8},{12,14},{14,12},{1,3},{3,1},... | collective-permute-start | bytes 393224 | tf_op jit(solution)/shard_map/ppermute | solution.py:410
  32.7 3.6 %shard_map.100.rest_0_ = bf16[128,4096]{1,0:T(8,128)(2,1)} custom-call(f32[2,16,2048]{2,1,0:T(8,128)S(1)} %get-tuple-element.58.enter_ref, f32[8,2,16,2048]{3,2,1,0:T(8,128)S(1)} %get-tuple-element.59.chunk_ref, f32[2,16,2048]{2,1,0:T(8,128)S(1)} %get-tuple-element.60.step_ref, f32[2,16,16,2048]{3,2,1,0:T(8,128)S(1)} %get-tuple-element.61.pow_ref, ...), custom_call_target="tpu_custom_call" | custom-call | flops 8388608 | bytes 8388608 | tf_op jit(solution)/shard_map/pallas_call | solution.py:392
  36.4 0.0 collective-permute-done.4.enter_ref
  36.4 3.6 %shard_map.101 = bf16[128,4096]{1,0:T(8,128)(2,1)} custom-call(bf16[2,16,2048]{2,1,0:T(8,128)(2,1)S(1)} %collective-permute-done.4.enter_ref, f32[8,2,16,2048]{3,2,1,0:T(8,128)S(1)} %get-tuple-element.54.chunk_ref, f32[2,16,2048]{2,1,0:T(8,128)S(1)} %get-tuple-element.55.step_ref, ...), custom_call_target="tpu_custom_call", output_to_operand_aliasing={{}: (6, {})} | custom-call | flops 8388608 | bytes 8388608 | tf_op jit(solution)/shard_map/pallas_call | solution.py:392
  (7 shorter events, 0.0 us)
Async XLA Ops:
  0.0 4.1 %copy-start.1 = (bf16[128,4096]{1,0:T(8,128)(2,1)S(1)}, bf16[128,4096]{1,0:T(8,128)(2,1)}, u32[]{:S(2)}) copy-start(bf16[128,4096]{1,0:T(8,128)(2,1)} %refs_1_.5) | copy-start | bytes 3145732
  0.0 4.1 %copy-start = (bf16[128,4096]{1,0:T(8,128)(2,1)S(1)}, bf16[128,4096]{1,0:T(8,128)(2,1)}, u32[]{:S(2)}) copy-start(bf16[128,4096]{1,0:T(8,128)(2,1)} %refs_0_.5) | copy-start | bytes 3145732
  0.0 4.1 %copy-start.3 = (bf16[3,7,4096]{2,1,0:T(8,128)(2,1)S(1)}, bf16[3,7,4096]{2,1,0:T(8,128)(2,1)}, u32[]{:S(2)}) copy-start(bf16[3,7,4096]{2,1,0:T(8,128)(2,1)} %taps_ref.5) | copy-start | bytes 516100
  0.0 4.1 %copy-start.7 = (f32[16,4096]{1,0:T(8,128)S(1)}, f32[16,4096]{1,0:T(8,128)}, u32[]{:S(2)}) copy-start(f32[16,4096]{1,0:T(8,128)} %refs_5_.1) | copy-start | bytes 786436
  0.0 4.1 %copy-start.6 = (f32[16,4096]{1,0:T(8,128)S(1)}, f32[16,4096]{1,0:T(8,128)}, u32[]{:S(2)}) copy-start(f32[16,4096]{1,0:T(8,128)} %refs_4_.3) | copy-start | bytes 786436
  1.1 11.0 %collective-permute-start = (bf16[3,8,4096]{2,1,0:T(8,128)(2,1)S(1)}, bf16[3,8,4096]{2,1,0:T(8,128)(2,1)S(1)}, u32[]{:S(2)}, u32[]{:S(2)}) collective-permute-start(bf16[3,8,4096]{2,1,0:T(8,128)(2,1)S(1)} %shard_map.91), channel_id=1, source_target_pairs={{0,2},{2,4},{4,6},{6,8},{8,10},{10,12},{12,14},{14,0},{1,3},{3,5},... | collective-permute-start | bytes 589832 | tf_op jit(solution)/shard_map/ppermute | solution.py:420
  13.2 5.4 %copy-start.2 = (bf16[128,4096]{1,0:T(8,128)(2,1)S(1)}, bf16[128,4096]{1,0:T(8,128)(2,1)}, u32[]{:S(2)}) copy-start(bf16[128,4096]{1,0:T(8,128)(2,1)} %q_ref.3) | copy-start | bytes 3145732
  13.2 5.4 %copy-start.4 = (f32[16,4096]{1,0:T(8,128)S(1)}, f32[16,4096]{1,0:T(8,128)}, u32[]{:S(2)}) copy-start(f32[16,4096]{1,0:T(8,128)} %res_re_ref.3) | copy-start | bytes 786436
  13.2 5.4 %copy-start.5 = (f32[16,4096]{1,0:T(8,128)S(1)}, f32[16,4096]{1,0:T(8,128)}, u32[]{:S(2)}) copy-start(f32[16,4096]{1,0:T(8,128)} %res_im_ref.3) | copy-start | bytes 786436
  13.2 5.4 %copy-start.8 = (f32[4096]{0:T(1024)S(1)}, f32[4096]{0:T(1024)}, u32[]{:S(2)}) copy-start(f32[4096]{0:T(1024)} %param.17) | copy-start | bytes 49156
  13.2 5.0 %collective-permute-start.1 = (bf16[2,16,2048]{2,1,0:T(8,128)(2,1)S(1)}, bf16[2,16,2048]{2,1,0:T(8,128)(2,1)S(1)}, u32[]{:S(2)}, u32[]{:S(2)}) collective-permute-start(bf16[2,16,2048]{2,1,0:T(8,128)(2,1)S(1)} %get-tuple-element.39), channel_id=1, source_target_pairs={{0,2},{2,0},{4,6},{6,4},{8,10},{10,8},{12,14},{14,12},{1,3},{3,1},... | collective-permute-start | bytes 393224 | tf_op jit(solution)/shard_map/ppermute | solution.py:410
  18.5 5.0 %collective-permute-start.2 = (bf16[2,16,2048]{2,1,0:T(8,128)(2,1)S(1)}, bf16[2,16,2048]{2,1,0:T(8,128)(2,1)S(1)}, u32[]{:S(2)}, u32[]{:S(2)}) collective-permute-start(bf16[2,16,2048]{2,1,0:T(8,128)(2,1)S(1)} %get-tuple-element.42), channel_id=1, source_target_pairs={{0,4},{2,6},{4,0},{6,2},{8,12},{10,14},{12,8},{14,10},{1,5},{3,7},... | collective-permute-start | bytes 393224 | tf_op jit(solution)/shard_map/ppermute | solution.py:410
  23.7 6.9 %collective-permute-start.3 = (bf16[2,16,2048]{2,1,0:T(8,128)(2,1)S(1)}, bf16[2,16,2048]{2,1,0:T(8,128)(2,1)S(1)}, u32[]{:S(2)}, u32[]{:S(2)}) collective-permute-start(bf16[2,16,2048]{2,1,0:T(8,128)(2,1)S(1)} %get-tuple-element.46), channel_id=1, source_target_pairs={{0,8},{2,10},{4,12},{6,14},{8,0},{10,2},{12,4},{14,6},{1,9},{3,11}... | collective-permute-start | bytes 393224 | tf_op jit(solution)/shard_map/ppermute | solution.py:410
  31.0 5.4 %collective-permute-start.4 = (bf16[2,16,2048]{2,1,0:T(8,128)(2,1)S(1)}, bf16[2,16,2048]{2,1,0:T(8,128)(2,1)S(1)}, u32[]{:S(2)}, u32[]{:S(2)}) collective-permute-start(bf16[2,16,2048]{2,1,0:T(8,128)(2,1)S(1)} %get-tuple-element.53), channel_id=1, source_target_pairs={{0,2},{2,0},{4,6},{6,4},{8,10},{10,8},{12,14},{14,12},{1,3},{3,1},... | collective-permute-start | bytes 393224 | tf_op jit(solution)/shard_map/ppermute | solution.py:410
